TPU v7x, 256 devices: a whole 4x4x8 slice. The times are simulated.
256 devices in a mesh: space: 128 (over x, y, z), rep: 2 (over core).
Axes of the slice: x: 4, y: 4, z: 8, core: 2. Of those that a mesh axis runs over, the one named last changes fastest.
Arguments:
- acts: bfloat16 [3072, 512, 128], P(('space', 'rep')), may hold values from -6 to 6
- preact: bfloat16 [3072, 512, 128], P(('space', 'rep')), may hold values from -8 to 8
- cotangent: bfloat16 [3072, 512, 128], P(('space', 'rep')), may hold values from -6 to 6
- filt: bfloat16 [3456, 128], P('space', 'rep'), may hold values from -0.109375 to 0.109375
- counts: int32 [256], replicated, may hold values from 1 to 12, as said below
- neighbors: int32 [3072, 27], P(('space', 'rep')), may hold values from 0 to 3072, as said below
Outputs:
- input_grad: bfloat16 [3072, 512, 128], P(('space', 'rep'))
- filt_grad: float32 [3456, 128], P('space', 'rep')
Inputs may be any that keep to these rules, and one draw needn't show every extreme that they name: counts[d] is the number of live bricks of device d, which fill its first slots; counts[d] + counts[d xor 1] <= 16, where d xor 1 is the other core of the same chip; in every draw some device holds 12 bricks and its partner 2 * 8 - 12. Brick n = d * 12 + s sits in slab d of the brick grid at one of 5 x 5 places, slot 0 of every device at the middle place; neighbors[n, k] is the index of the live brick at offset off_k (first component along the slabs, so it lies on device d - 1, d or d + 1) from that place, or 3072 where there is none, also for bricks that are not live.
All inputs are finite; a program needn't handle non-finite values.
Results may differ from a plain program's by a relative error of at most 0.0049.
Values may be sent and summed in bfloat16 or wider, within the bound.
A program may use at most 128 MiB of HBM per device.

v0:
```python
import math

import jax
import jax.numpy as jnp
from jax import lax
from jax.sharding import PartitionSpec as P

BRICK = 8


tap_offsets = [
    (step_x, step_y, step_z)
    for step_x in (-1, 0, 1)
    for step_y in (-1, 0, 1)
    for step_z in (-1, 0, 1)
]


def shifted(x, axis, by):
    count = lax.axis_size(axis)
    pairs = [(i, i + by) for i in range(count) if 0 <= i + by < count]
    return lax.ppermute(x, axis, pairs)


def silu_slope(values):
    sigma = jax.nn.sigmoid(values)
    return sigma * (1.0 + values * (1.0 - sigma))


def edge(offset, brick_side):
    if offset < 0:
        return slice(brick_side - 1, brick_side)
    if offset == 0:
        return slice(0, brick_side)
    return slice(0, 1)


def assemble(planes, indices, usable):
    layers = []
    for step_x in range(3):
        strips = []
        for step_y in range(3):
            columns = []
            for step_z in range(3):
                tap = step_x * 9 + step_y * 3 + step_z
                source = planes[step_x]
                brick_side = source.shape[2]
                fetched = jnp.take(source, indices[:, tap], axis=0)
                fetched = fetched[:, :, edge(step_y - 1, brick_side), edge(step_z - 1, brick_side)]
                keeper = usable[:, tap][:, None, None, None, None]
                columns.append(jnp.where(keeper, fetched, jnp.zeros_like(fetched)))
            strips.append(jnp.concatenate(columns, axis=3))
        layers.append(jnp.concatenate(strips, axis=2))
    return jnp.concatenate(layers, axis=1)


def unfold(padded, direction):
    brick_side = padded.shape[0] - 2
    sections = []
    for step_x, step_y, step_z in tap_offsets:
        start_x = 1 + direction * step_x
        start_y = 1 + direction * step_y
        start_z = 1 + direction * step_z
        sections.append(
            padded[
                start_x : start_x + brick_side,
                start_y : start_y + brick_side,
                start_z : start_z + brick_side,
            ]
        )
    return jnp.concatenate(sections, axis=-1).reshape(brick_side**3, -1)


def run_bricks(act_pad, grad_pad, filt_flip, running):

    def per_brick(accum, operands):
        act_block, grad_block = operands
        unrolled_act = unfold(act_block, 1)
        unrolled_grad = unfold(grad_block, -1)
        center = grad_block[1:-1, 1:-1, 1:-1].reshape(-1, grad_block.shape[-1])
        accum = accum + lax.dot_general(
            unrolled_act, center, (((0,), (0,)), ((), ())), preferred_element_type=jnp.float32
        )
        return (accum, jnp.dot(unrolled_grad, filt_flip, preferred_element_type=jnp.float32))

    return lax.scan(per_brick, running, (act_pad, grad_pad))


def on_device(acts, preact, cotangent, filt, counts, neighbors):
    slot_count, voxels, channels = acts.shape
    devices = lax.axis_size(("space", "rep"))
    position = lax.axis_index(("space", "rep"))
    grand_total = slot_count * devices
    live_count = counts[position]
    is_live = jnp.arange(slot_count) < live_count
    grad_pre = jnp.where(
        is_live[:, None, None],
        cotangent.astype(jnp.float32) * silu_slope(preact.astype(jnp.float32)),
        0.0,
    ).astype(jnp.bfloat16)
    gathered_rows = lax.all_gather(filt, "space", axis=0, tiled=True)
    full_filter = lax.all_gather(gathered_rows, "rep", axis=1, tiled=True)
    filt_flip = (
        full_filter.reshape(27, channels, channels)
        .transpose(0, 2, 1)
        .reshape(27 * channels, channels)
    )
    act_five = acts.reshape(slot_count, BRICK, BRICK, BRICK, channels)
    grad_five = grad_pre.reshape(slot_count, BRICK, BRICK, BRICK, channels)
    from_below = shifted((act_five[:, BRICK - 1 :], grad_five[:, BRICK - 1 :]), ("space", "rep"), 1)
    from_above = shifted((act_five[:, :1], grad_five[:, :1]), ("space", "rep"), -1)
    usable = neighbors < grand_total
    slab_step = jnp.arange(27, dtype=jnp.int32) // 9 - 1
    local_slot = jnp.clip(
        neighbors - (position + slab_step[None, :]) * slot_count, 0, slot_count - 1
    )
    act_pad = assemble((from_below[0], act_five, from_above[0]), local_slot, usable)
    grad_pad = assemble((from_below[1], grad_five, from_above[1]), local_slot, usable)
    start = jnp.zeros((27 * channels, channels), jnp.float32)
    filt_sum, grads = run_bricks(act_pad, grad_pad, filt_flip, start)
    brick_grads = grads.astype(jnp.bfloat16)
    input_grad = jnp.where(is_live[:, None, None], brick_grads, jnp.zeros_like(brick_grads))
    inverse_norm = 1.0 / math.sqrt(grand_total * voxels)
    shard_rows = lax.psum_scatter(filt_sum, "space", scatter_dimension=0, tiled=True)
    filt_grad = lax.psum_scatter(shard_rows, "rep", scatter_dimension=1, tiled=True)
    return (input_grad, filt_grad * inverse_norm)


def solution(mesh):
    in_specs = (
        P(("space", "rep"), None, None),
        P(("space", "rep"), None, None),
        P(("space", "rep"), None, None),
        P("space", "rep"),
        P(),
        P(("space", "rep"), None),
    )
    out_specs = (P(("space", "rep"), None, None), P("space", "rep"))
    return jax.shard_map(
        on_device, mesh=mesh, in_specs=in_specs, out_specs=out_specs, check_vma=False
    )
```

profile of v0, /device:TPU:1, one launch (start us, length us, event | category | flops | bytes accessed | tf_op | source)
XLA Modules:
  0.0 1390.8 jit_solution(1618855230662512076)
XLA Ops:
  9.3 3.3 fusion.11
  13.4 5.1 collective-permute-start.3
  21.2 3.6 collective-permute-start.2
  112.0 295.4 %all-gather = bf16[128,27,64]{2,1,0:T(8,128)(2,1)S(1)} all-gather(bf16[1,27,64]{2,1,0:T(8,128)(2,1)S(1)} %bitcast.211), channel_id=1, replica_groups=mesh['space'=128,'rep'=2] {'space'}, dimensions={0}, use_global_device_ids=true | all-gather | bytes 445824 | tf_op jit(solution)/shard_map/all_gather | solution.py:101
  408.1 58.8 %all_gather.7 = bf16[3456,128]{0,1:T(8,128)(2,1)S(1)} all-gather(bf16[3456,64]{0,1:T(8,128)(2,1)S(1)} %copy.9), channel_id=1, replica_groups=mesh['space'=128,'rep'=2] {'rep'}, dimensions={1}, use_global_device_ids=true | all-gather | bytes 1327104 | tf_op jit(solution)/shard_map/all_gather | solution.py:102
  469.3 3.5 select_select_fusion
  472.9 4.8 broadcast_select_fusion.4
  477.7 2.3 fusion.12
  480.0 2.2 broadcast_select_fusion.32
  482.2 2.2 broadcast_select_fusion.28
  487.5 2.2 gather_fusion.21
  496.5 2.2 gather_fusion.25
  499.9 2.2 gather_fusion.18
  503.4 2.2 gather_fusion.20
  510.2 2.2 gather_fusion.26
  523.9 2.2 gather_fusion.1
  537.6 2.2 gather_fusion.22
  541.2 2.3 gather_fusion.4
  544.8 2.2 gather_fusion.2
  559.2 8.8 maximum_maximum_fusion.1
  568.0 6.8 maximum_maximum_fusion
  574.8 353.8 %while.14 = (s32[]{:T(128)}, f32[3456,128]{1,0:T(8,128)}, bf16[12,512,128]{2,1,0:T(8,128)(2,1)}, bf16[12,10,10,10,128]{4,3,2,1,0:T(8,128)(2,1)}, bf16[12,10,10,1...) while((s32[]{:T(128)}, f32[3456,128]{1,0:T(8,128)}, ...), condition=%wide.region_1.4_spmd.clone.clone, body=%wide.region_0.3_spmd.clone.sunk.clone | while | flops 906854400 | bytes 41230984 | solution.py:86
  598.9 4.2 fusion.52
  628.4 4.2 fusion.52
  657.9 4.2 fusion.52
  687.4 4.2 fusion.52
  716.8 4.2 fusion.52
  746.3 4.2 fusion.52
  775.8 4.2 fusion.52
  805.3 4.2 fusion.52
  834.8 4.2 fusion.52
  864.2 4.2 fusion.52
  893.7 4.2 fusion.52
  923.2 4.2 fusion.52
  928.6 296.9 %fusion = f32[32,128]{1,0:T(8,128)S(1)} fusion(f32[3456,128]{1,0:T(8,128)} %get-tuple-element.38), kind=kCustom, calls=%all-reduce-scatter | all-reduce-scatter fusion | flops 524289 | bytes 1786880
  1234.1 7.0 collective-permute-start.15
  1243.7 5.8 collective-permute-start.18
  1249.5 22.4 %collective-permute-start.19 = (f32[32,128]{1,0:T(8,128)S(1)}, f32[32,128]{1,0:T(8,128)S(1)}, u32[]{:S(2)}, u32[]{:S(2)}) collective-permute-start(f32[32,128]{1,0:T(8,128)S(1)} %fusion), channel_id=1, source_target_pairs={{0,32},{2,34},{4,36},{6,38},{8,40},{10,42},{12,44},{14,46},{16,48}... | collective-permute-start | bytes 49160
  1272.0 2.5 collective-permute-start.20
  1274.5 7.8 collective-permute-start.21
  1282.4 4.9 collective-permute-start.22
  1287.3 2.2 collective-permute-start.4
  1291.5 4.6 collective-permute-start.6
  1296.1 4.3 collective-permute-start.7
  1300.4 4.0 collective-permute-start.8
  1304.4 2.2 collective-permute-start.9
  1308.0 2.6 concatenate.112
  1312.7 69.8 %reduce-scatter.6.cloned.1.call-done = f32[64,27]{1,0:T(8,128)} async-done(((f32[128,27]{1,0:T(8,128)}), f32[64,27]{1,0:T(8,128)}) %reduce-scatter.6.cloned.1.call-update) | async-done | bytes 6928
  (1006 shorter events, 468.9 us)
Async XLA Ops:
  7.2 19.6 %copy-start.14 = (s32[12,27]{1,0:T(8,128)S(1)}, s32[12,27]{1,0:T(8,128)}, u32[]{:S(2)}) copy-start(s32[12,27]{1,0:T(8,128)} %param.17) | copy-start | bytes 3892
  7.2 1375.3 %reduce-scatter.6.cloned.1.call-start = ((), (), s32[]{:S(2)}) async-start(), calls=%async_computation.1 | async-start | bytes 98304
  7.2 22.8 %copy-start.15 = (s32[12,27]{1,0:T(8,128)S(1)}, s32[12,27]{1,0:T(8,128)}, u32[]{:S(2)}) copy-start(s32[12,27]{1,0:T(8,128)} %param.17) | copy-start | bytes 3892
  13.4 471.6 %collective-permute-start.3 = (bf16[12,1,8,8,128]{4,3,2,1,0:T(8,128)(2,1)}, bf16[12,1,8,8,128]{4,3,2,1,0:T(8,128)(2,1)S(1)}, u32[]{:S(2)}, u32[]{:S(2)}) collective-permute-start(bf16[12,1,8,8,128]{4,3,2,1,0:T(8,128)(2,1)} %get-tuple-element.129), channel_id=1, source_target_pairs={{1,0},{2,1},{3,2},{4,3},{5,4},{6,5},{7,6},{8,7},{9,8},{10,9},{11,1... | collective-permute-start | bytes 589832 | tf_op jit(solution)/shard_map/ppermute | solution.py:22
  19.3 468.2 %collective-permute-start.1 = (bf16[12,1,8,8,128]{4,3,2,1,0:T(8,128)(2,1)}, bf16[12,1,8,8,128]{4,3,2,1,0:T(8,128)(2,1)}, u32[]{:S(2)}, u32[]{:S(2)}) collective-permute-start(bf16[12,1,8,8,128]{4,3,2,1,0:T(8,128)(2,1)} %get-tuple-element.131), channel_id=1, source_target_pairs={{1,0},{2,1},{3,2},{4,3},{5,4},{6,5},{7,6},{8,7},{9,8},{10,9},{11,1... | collective-permute-start | bytes 589832 | tf_op jit(solution)/shard_map/ppermute | solution.py:22
  21.2 491.2 %collective-permute-start.2 = (bf16[12,1,8,8,128]{4,3,2,1,0:T(8,128)(2,1)}, bf16[12,1,8,8,128]{4,3,2,1,0:T(8,128)(2,1)S(1)}, u32[]{:S(2)}, u32[]{:S(2)}) collective-permute-start(bf16[12,1,8,8,128]{4,3,2,1,0:T(8,128)(2,1)} %get-tuple-element.128), channel_id=1, source_target_pairs={{0,1},{1,2},{2,3},{3,4},{4,5},{5,6},{6,7},{7,8},{8,9},{9,10},{10,1... | collective-permute-start | bytes 589832 | tf_op jit(solution)/shard_map/ppermute | solution.py:22
  24.8 490.1 %collective-permute-start = (bf16[12,1,8,8,128]{4,3,2,1,0:T(8,128)(2,1)}, bf16[12,1,8,8,128]{4,3,2,1,0:T(8,128)(2,1)}, u32[]{:S(2)}, u32[]{:S(2)}) collective-permute-start(bf16[12,1,8,8,128]{4,3,2,1,0:T(8,128)(2,1)} %get-tuple-element.130), channel_id=1, source_target_pairs={{0,1},{1,2},{2,3},{3,4},{4,5},{5,6},{6,7},{7,8},{8,9},{9,10},{10,1... | collective-permute-start | bytes 589832 | tf_op jit(solution)/shard_map/ppermute | solution.py:22
  82.4 29.6 %copy-start.29 = (s32[12]{0:T(128)}, s32[12]{0:T(128)S(1)}, u32[]{:S(2)}) copy-start(s32[12]{0:T(128)S(1)} %get-tuple-element.86) | copy-start | bytes 148
  82.4 29.6 %copy-start.16 = (bf16[27,64]{1,0:T(8,128)(2,1)S(1)}, bf16[27,64]{1,0:T(8,128)(2,1)}, u32[]{:S(2)}) copy-start(bf16[27,64]{1,0:T(8,128)(2,1)} %param.15) | copy-start | bytes 10372
  407.7 61.5 %copy-start.35 = (pred[12]{0:T(512)(128)(4,1)S(1)}, pred[12]{0:T(512)(128)(4,1)}, u32[]{:S(2)}) copy-start(pred[12]{0:T(512)(128)(4,1)} %get-tuple-element.101) | copy-start | bytes 40
  407.7 61.5 %copy-start.36 = (pred[12]{0:T(512)(128)(4,1)S(1)}, pred[12]{0:T(512)(128)(4,1)}, u32[]{:S(2)}) copy-start(pred[12]{0:T(512)(128)(4,1)} %get-tuple-element.202) | copy-start | bytes 40
  522.7 28.5 %copy-start.21 = (pred[12]{0:T(512)(128)(4,1)S(1)}, pred[12]{0:T(512)(128)(4,1)}, u32[]{:S(2)}) copy-start(pred[12]{0:T(512)(128)(4,1)} %get-tuple-element.91) | copy-start | bytes 40
  522.7 28.5 %copy-start.22 = (pred[12]{0:T(512)(128)(4,1)S(1)}, pred[12]{0:T(512)(128)(4,1)}, u32[]{:S(2)}) copy-start(pred[12]{0:T(512)(128)(4,1)} %get-tuple-element.93) | copy-start | bytes 40
  523.9 28.8 %copy-start.19 = (pred[12]{0:T(512)(128)(4,1)S(1)}, pred[12]{0:T(512)(128)(4,1)}, u32[]{:S(2)}) copy-start(pred[12]{0:T(512)(128)(4,1)} %get-tuple-element.89) | copy-start | bytes 40
  523.9 28.9 %copy-start.20 = (pred[12]{0:T(512)(128)(4,1)S(1)}, pred[12]{0:T(512)(128)(4,1)}, u32[]{:S(2)}) copy-start(pred[12]{0:T(512)(128)(4,1)} %get-tuple-element.95) | copy-start | bytes 40
  526.1 28.6 %copy-start.17 = (pred[12]{0:T(512)(128)(4,1)S(1)}, pred[12]{0:T(512)(128)(4,1)}, u32[]{:S(2)}) copy-start(pred[12]{0:T(512)(128)(4,1)} %get-tuple-element.88) | copy-start | bytes 40
  526.1 28.6 %copy-start.18 = (pred[12]{0:T(512)(128)(4,1)S(1)}, pred[12]{0:T(512)(128)(4,1)}, u32[]{:S(2)}) copy-start(pred[12]{0:T(512)(128)(4,1)} %get-tuple-element.90) | copy-start | bytes 40
  537.6 21.4 %copy-start.5 = (bf16[12,8,8,1,128]{4,3,2,1,0:T(2,128)(2,1)S(1)}, bf16[12,8,8,1,128]{4,3,2,1,0:T(2,128)(2,1)}, u32[]{:S(2)}) copy-start(bf16[12,8,8,1,128]{4,3,2,1,0:T(2,128)(2,1)} %get-tuple-element.160) | copy-start | bytes 589828
  574.8 731.8 %copy-start.46 = (u32[256]{0:T(256)S(1)}, u32[256]{0:T(256)}, u32[]{:S(2)}) copy-start(u32[256]{0:T(256)} %constant.87) | copy-start | bytes 3076
  574.8 736.5 %copy-start.32 = (pred[12]{0:T(512)(128)(4,1)S(1)}, pred[12]{0:T(512)(128)(4,1)}, u32[]{:S(2)}) copy-start(pred[12]{0:T(512)(128)(4,1)} %copy-done.31) | copy-start | bytes 40
  609.1 19.3 %copy-start.2 = (f32[3456,128]{1,0:T(8,128)S(1)}, f32[3456,128]{1,0:T(8,128)}, u32[]{:S(2)}) copy-start(f32[3456,128]{1,0:T(8,128)} %get-tuple-element.277) | copy-start | bytes 5308420 | tf_op jit(solution)/shard_map/while
  638.6 19.3 %copy-start.2 = (f32[3456,128]{1,0:T(8,128)S(1)}, f32[3456,128]{1,0:T(8,128)}, u32[]{:S(2)}) copy-start(f32[3456,128]{1,0:T(8,128)} %get-tuple-element.277) | copy-start | bytes 5308420 | tf_op jit(solution)/shard_map/while
  668.0 19.3 %copy-start.2 = (f32[3456,128]{1,0:T(8,128)S(1)}, f32[3456,128]{1,0:T(8,128)}, u32[]{:S(2)}) copy-start(f32[3456,128]{1,0:T(8,128)} %get-tuple-element.277) | copy-start | bytes 5308420 | tf_op jit(solution)/shard_map/while
  697.5 19.3 %copy-start.2 = (f32[3456,128]{1,0:T(8,128)S(1)}, f32[3456,128]{1,0:T(8,128)}, u32[]{:S(2)}) copy-start(f32[3456,128]{1,0:T(8,128)} %get-tuple-element.277) | copy-start | bytes 5308420 | tf_op jit(solution)/shard_map/while
  727.0 19.3 %copy-start.2 = (f32[3456,128]{1,0:T(8,128)S(1)}, f32[3456,128]{1,0:T(8,128)}, u32[]{:S(2)}) copy-start(f32[3456,128]{1,0:T(8,128)} %get-tuple-element.277) | copy-start | bytes 5308420 | tf_op jit(solution)/shard_map/while
  756.5 19.3 %copy-start.2 = (f32[3456,128]{1,0:T(8,128)S(1)}, f32[3456,128]{1,0:T(8,128)}, u32[]{:S(2)}) copy-start(f32[3456,128]{1,0:T(8,128)} %get-tuple-element.277) | copy-start | bytes 5308420 | tf_op jit(solution)/shard_map/while
  786.0 19.3 %copy-start.2 = (f32[3456,128]{1,0:T(8,128)S(1)}, f32[3456,128]{1,0:T(8,128)}, u32[]{:S(2)}) copy-start(f32[3456,128]{1,0:T(8,128)} %get-tuple-element.277) | copy-start | bytes 5308420 | tf_op jit(solution)/shard_map/while
  928.6 382.7 %copy-start.6 = (bf16[12,512,128]{2,1,0:T(8,128)(2,1)S(1)}, bf16[12,512,128]{2,1,0:T(8,128)(2,1)}, u32[]{:S(2)}) copy-start(bf16[12,512,128]{2,1,0:T(8,128)(2,1)} %get-tuple-element.37) | copy-start | bytes 4718596
  1225.5 8.6 collective-permute-start.10
  1226.8 14.3 %collective-permute-start.11 = (f32[32,128]{1,0:T(8,128)S(1)}, f32[32,128]{1,0:T(8,128)S(1)}, u32[]{:S(2)}, u32[]{:S(2)}) collective-permute-start(f32[32,128]{1,0:T(8,128)S(1)} %fusion), channel_id=1, source_target_pairs={{0,16},{2,18},{4,20},{6,22},{8,24},{10,26},{12,28},{14,30},{16,32}... | collective-permute-start | bytes 49160
  1228.1 14.3 %collective-permute-start.12 = (f32[32,128]{1,0:T(8,128)S(1)}, f32[32,128]{1,0:T(8,128)S(1)}, u32[]{:S(2)}, u32[]{:S(2)}) collective-permute-start(f32[32,128]{1,0:T(8,128)S(1)} %fusion), channel_id=1, source_target_pairs={{0,18},{2,20},{4,22},{6,24},{8,26},{10,28},{12,30},{14,32},{16,34}... | collective-permute-start | bytes 49160
  1229.4 14.3 %collective-permute-start.13 = (f32[32,128]{1,0:T(8,128)S(1)}, f32[32,128]{1,0:T(8,128)S(1)}, u32[]{:S(2)}, u32[]{:S(2)}) collective-permute-start(f32[32,128]{1,0:T(8,128)S(1)} %fusion), channel_id=1, source_target_pairs={{0,20},{2,22},{4,24},{6,26},{8,28},{10,30},{12,32},{14,34},{16,36}... | collective-permute-start | bytes 49160
  1230.7 2.1 collective-permute-start.23
  1232.8 16.7 %collective-permute-start.14 = (f32[32,128]{1,0:T(8,128)S(1)}, f32[32,128]{1,0:T(8,128)S(1)}, u32[]{:S(2)}, u32[]{:S(2)}) collective-permute-start(f32[32,128]{1,0:T(8,128)S(1)} %fusion), channel_id=1, source_target_pairs={{0,22},{2,24},{4,26},{6,28},{8,30},{10,32},{12,34},{14,36},{16,38}... | collective-permute-start | bytes 49160
  1234.1 37.8 %collective-permute-start.15 = (f32[32,128]{1,0:T(8,128)S(1)}, f32[32,128]{1,0:T(8,128)S(1)}, u32[]{:S(2)}, u32[]{:S(2)}) collective-permute-start(f32[32,128]{1,0:T(8,128)S(1)} %fusion), channel_id=1, source_target_pairs={{0,24},{2,26},{4,28},{6,30},{8,32},{10,34},{12,36},{14,38},{16,40}... | collective-permute-start | bytes 49160
  1241.1 33.4 %collective-permute-start.16 = (f32[32,128]{1,0:T(8,128)S(1)}, f32[32,128]{1,0:T(8,128)S(1)}, u32[]{:S(2)}, u32[]{:S(2)}) collective-permute-start(f32[32,128]{1,0:T(8,128)S(1)} %fusion), channel_id=1, source_target_pairs={{0,26},{2,28},{4,30},{6,32},{8,34},{10,36},{12,38},{14,40},{16,42}... | collective-permute-start | bytes 49160
  1242.4 40.0 %collective-permute-start.17 = (f32[32,128]{1,0:T(8,128)S(1)}, f32[32,128]{1,0:T(8,128)S(1)}, u32[]{:S(2)}, u32[]{:S(2)}) collective-permute-start(f32[32,128]{1,0:T(8,128)S(1)} %fusion), channel_id=1, source_target_pairs={{0,28},{2,30},{4,32},{6,34},{8,36},{10,38},{12,40},{14,42},{16,44}... | collective-permute-start | bytes 49160
  1243.7 43.6 %collective-permute-start.18 = (f32[32,128]{1,0:T(8,128)S(1)}, f32[32,128]{1,0:T(8,128)S(1)}, u32[]{:S(2)}, u32[]{:S(2)}) collective-permute-start(f32[32,128]{1,0:T(8,128)S(1)} %fusion), channel_id=1, source_target_pairs={{0,30},{2,32},{4,34},{6,36},{8,38},{10,40},{12,42},{14,44},{16,46}... | collective-permute-start | bytes 49160
  1249.5 40.0 %collective-permute-start.19 = (f32[32,128]{1,0:T(8,128)S(1)}, f32[32,128]{1,0:T(8,128)S(1)}, u32[]{:S(2)}, u32[]{:S(2)}) collective-permute-start(f32[32,128]{1,0:T(8,128)S(1)} %fusion), channel_id=1, source_target_pairs={{0,32},{2,34},{4,36},{6,38},{8,40},{10,42},{12,44},{14,46},{16,48}... | collective-permute-start | bytes 49160
  1272.0 19.5 %collective-permute-start.20 = (f32[32,128]{1,0:T(8,128)S(1)}, f32[32,128]{1,0:T(8,128)S(1)}, u32[]{:S(2)}, u32[]{:S(2)}) collective-permute-start(f32[32,128]{1,0:T(8,128)S(1)} %fusion), channel_id=1, source_target_pairs={{0,34},{2,36},{4,38},{6,40},{8,42},{10,44},{12,46},{14,48},{16,50}... | collective-permute-start | bytes 49160
  1274.5 21.5 %collective-permute-start.21 = (f32[32,128]{1,0:T(8,128)S(1)}, f32[32,128]{1,0:T(8,128)S(1)}, u32[]{:S(2)}, u32[]{:S(2)}) collective-permute-start(f32[32,128]{1,0:T(8,128)S(1)} %fusion), channel_id=1, source_target_pairs={{0,36},{2,38},{4,40},{6,42},{8,44},{10,46},{12,48},{14,50},{16,52}... | collective-permute-start | bytes 49160
  1282.4 18.0 %collective-permute-start.22 = (f32[32,128]{1,0:T(8,128)S(1)}, f32[32,128]{1,0:T(8,128)S(1)}, u32[]{:S(2)}, u32[]{:S(2)}) collective-permute-start(f32[32,128]{1,0:T(8,128)S(1)} %fusion), channel_id=1, source_target_pairs={{0,38},{2,40},{4,42},{6,44},{8,46},{10,48},{12,50},{14,52},{16,54}... | collective-permute-start | bytes 49160
  1287.3 17.1 %collective-permute-start.4 = (f32[32,128]{1,0:T(8,128)S(1)}, f32[32,128]{1,0:T(8,128)S(1)}, u32[]{:S(2)}, u32[]{:S(2)}) collective-permute-start(f32[32,128]{1,0:T(8,128)S(1)} %fusion), channel_id=1, source_target_pairs={{0,2},{2,4},{4,6},{6,8},{8,10},{10,12},{12,14},{14,16},{16,18},{18... | collective-permute-start | bytes 49160
  1289.5 18.4 %collective-permute-start.5 = (f32[32,128]{1,0:T(8,128)S(1)}, f32[32,128]{1,0:T(8,128)S(1)}, u32[]{:S(2)}, u32[]{:S(2)}) collective-permute-start(f32[32,128]{1,0:T(8,128)S(1)} %fusion), channel_id=1, source_target_pairs={{0,4},{2,6},{4,8},{6,10},{8,12},{10,14},{12,16},{14,18},{16,20},{1... | collective-permute-start | bytes 49160
  1291.5 16.4 %collective-permute-start.6 = (f32[32,128]{1,0:T(8,128)S(1)}, f32[32,128]{1,0:T(8,128)S(1)}, u32[]{:S(2)}, u32[]{:S(2)}) collective-permute-start(f32[32,128]{1,0:T(8,128)S(1)} %fusion), channel_id=1, source_target_pairs={{0,6},{2,8},{4,10},{6,12},{8,14},{10,16},{12,18},{14,20},{16,22},{... | collective-permute-start | bytes 49160
  1296.1 11.9 collective-permute-start.7
  1300.4 7.5 collective-permute-start.8
  1304.4 3.5 collective-permute-start.9
  (46 other events, 349.5 us)
Sparse Core Ops, SparseCore 0:
  1311.4 71.0 reduce-scatter.5
where the time goes:
time: 1390 us
  blocking collectives  651 us (47%)
  local copies, waits for them, and re-layouts  392 us (28%)
  other arithmetic  94.9 us (7%)
  starting transfers between devices  92.6 us (7%)
  matrix products  71.2 us (5%)
  waiting for transfers between devices  70.8 us (5%)
  between operations  15.7 us (1%)
    unnamed x1, blocking collectives  297 us
    all_gather x1, blocking collectives, on_device(): gathered_rows = lax.all_gather(filt, 'space', axis=0, tiled=True)  295 us
    while x672, local copies, waits for them, and re-layouts  256 us
    gather x54, local copies, waits for them, and re-layouts, assemble(): fetched = jnp.take(source, indices[:, tap], axis=0)  97.3 us
    unnamed x21, starting transfers between devices  80 us
    unnamed x22, waiting for transfers between devices  70.8 us
    all_gather x1, blocking collectives, on_device(): full_filter = lax.all_gather(gathered_rows, 'rep', axis=1, tiled=True)  58.8 us
    dot_general x12, matrix products, per_brick(): lax.dot_general(unrolled_act, center, (((0,), (0,)), ((), ())), preferred...  50.3 us
  transfers between devices with their start and end apart: 25, of which 2 were waited for; matrix products, arithmetic and copies ran while one was open for 10% of the time, Pallas kernels for 0%

commit v1 on v0

v1 whole, which is shorter than its diff:
```python
import math

import jax
import jax.numpy as jnp
from jax import lax
from jax.experimental import pallas as pl
from jax.experimental.pallas import tpu as pltpu
from jax.sharding import PartitionSpec as P


SLOTS = 12
VOX = 512
C = 128
DEVICES = 256
CHIPS = 128
BRICKS = SLOTS * DEVICES
F32 = jnp.float32
BF16 = jnp.bfloat16
MESH = pl.DeviceIdType.MESH
SEGMENTS = 3


def slope_times(cotangent, preact):
    values = preact.astype(F32)
    sigma = 1.0 / (1.0 + jnp.exp(-values))
    return cotangent.astype(F32) * (sigma * (1.0 + values * (1.0 - sigma)))


def kernel(
    counts, neighbors, acts_hbm, pre_hbm, cot_hbm, filt_ref, in_grad_hbm, filt_grad_ref,
    acts, pre, cot, grads, halo_out, halo_in, halo, pads, acts_t, weights, filt_sum, filt_full,
    own_rows, pair_rows, rows, rs_pair, rs_pair_in, sum1, send1, recv1, sum2, send2, recv2,
    send3, recv3, sum4, recv4, in_grad, load_sem, store_sem, halo_sems, pair_sems, gz_sems, g2_sems,
    g1_sems, gp_sems, rp_sems, r1_sems, r2_sems, r3_sems, r4_sems,
):
    chip = lax.axis_index("space")
    core = lax.axis_index("rep")
    device = chip * 2 + core
    z = chip % 8
    stride1 = 32 - 24 * core
    stride2 = 8 + 24 * core
    c1 = (chip // stride1) % 4
    c2 = (chip // stride2) % 4

    def to(chip_id, core_id):
        return {"space": chip_id, "rep": core_id}

    partner = to(chip, 1 - core)
    above = (device + 1) % DEVICES
    below = (device + DEVICES - 1) % DEVICES
    outer = (device + DEVICES - 1 + 2 * core) % DEVICES

    def peer1(t):
        return to(chip + ((c1 + t) % 4 - c1) * stride1, core)

    def peer2(t):
        return to(chip + ((c2 + t) % 4 - c2) * stride2, core)

    def peerz(t):
        return to(chip + (z + t) % 8 - z, core)

    def load(source, target, part, index):
        span = pl.ds(part * 4, 4)
        return pltpu.make_async_copy(source.at[span], target.at[span], load_sem.at[index * 3 + part])

    loads = [load(s, t, part, i) for i, (s, t) in enumerate(((pre_hbm, pre), (cot_hbm, cot), (acts_hbm, acts))) for part in range(3)]
    for item in loads:
        item.start()

    barrier = pltpu.get_barrier_semaphore()
    greeted = [partner, to(outer // 2, outer % 2)]
    greeted += [peerz(t) for t in range(1, 8)] + [peer1(t) for t in range(1, 4)] + [peer2(t) for t in range(1, 4)]
    for other in greeted:
        pl.semaphore_signal(barrier, inc=1, device_id=other, device_id_type=MESH)

    def remote(source, target, sems, index, other):
        return pltpu.make_async_remote_copy(
            src_ref=source, dst_ref=target, send_sem=sems.at[0, index], recv_sem=sems.at[1, index],
            device_id=other, device_id_type=MESH,
        )

    started = []

    def go(copies):
        for item in copies:
            item.start()
        started.extend(copies)
        return copies

    def arrive(copies):
        for item in copies:
            item.wait_recv()

    wide = jnp.concatenate([filt_ref[...].astype(F32), jnp.zeros((27, 64), F32)], axis=1)
    wide = jnp.where(core == 0, wide, pltpu.roll(wide, 64, 1))
    filt_sum[0:32, :] = jnp.zeros((32, C), F32)
    filt_sum[0:27, :] = wide
    own_rows[...] = filt_sum[0:32, :].astype(BF16)
    filt_sum[3456:3464, :] = jnp.zeros((8, C), F32)
    grads[SLOTS] = jnp.zeros((8, 8, 8, C), F32)
    halo[0, SLOTS] = jnp.zeros((1, 8, 8, C), F32)
    halo[1, SLOTS] = jnp.zeros((1, 8, 8, C), F32)

    for item in loads[:6]:
        item.wait()
    live_count = counts[device]

    def outer_layers(b, carry):
        for side, x in ((0, 0), (1, 7)):
            g = slope_times(cot[b, x * 64:(x + 1) * 64, :], pre[b, x * 64:(x + 1) * 64, :])
            g = jnp.where(b < live_count, g, 0.0)
            grads[b, x] = g.reshape(8, 8, C)
            halo_out[side, b] = g.astype(BF16)
        return carry

    lax.fori_loop(0, SLOTS, outer_layers, 0)
    pl.semaphore_wait(barrier, len(greeted))
    halos = go([
        remote(halo_out.at[0], halo_in.at[1], halo_sems, 0, to(below // 2, below % 2)),
        remote(halo_out.at[1], halo_in.at[0], halo_sems, 1, to(above // 2, above % 2)),
    ])
    gather_pair = go([remote(own_rows, pair_rows, pair_sems, 0, partner)])

    def inner_layers(b, carry):
        for x in range(1, 7):
            g = slope_times(cot[b, x * 64:(x + 1) * 64, :], pre[b, x * 64:(x + 1) * 64, :])
            grads[b, x] = jnp.where(b < live_count, g, 0.0).reshape(8, 8, C)
        return carry

    lax.fori_loop(0, SLOTS, inner_layers, 0)
    for item in loads[6:]:
        item.wait()

    arrive(gather_pair)
    chunk = own_rows[...].astype(F32) + pair_rows[...].astype(F32)
    rows[core, c1, c2, z] = jnp.where(core == 0, chunk[0:16], chunk[16:32]).astype(BF16)
    here = rows.at[core, c1, c2, z]
    gather_z = go([remote(here, here, gz_sems, t, peerz(t)) for t in range(1, 8)])

    def transpose_acts(b, carry):
        a = acts[b].astype(F32).reshape(32, 2, 8, C)
        span = pl.ds(pl.multiple_of(b * 256, 256), 256)
        for parity in range(2):
            acts_t[parity * C:(parity + 1) * C, span] = a[:, parity].reshape(256, C).T.astype(BF16)
        return carry

    lax.fori_loop(0, SLOTS, transpose_acts, 0)

    row = lax.broadcasted_iota(jnp.int32, (1, 8, C), 1)

    def assemble(b, source, layer, x_from, count, x_to):
        def slot(step_y, step_z):
            index = neighbors[b, layer * 9 + (step_y + 1) * 3 + step_z + 1]
            local = jnp.clip(index - (device + layer - 1) * SLOTS, 0, SLOTS - 1)
            return jnp.where((index < BRICKS) & (b < live_count), local, SLOTS)

        slots = {(sy, sz): slot(sy, sz) for sy in (-1, 0, 1) for sz in (-1, 0, 1)}
        for lane in range(2):
            tiles = []
            for pair in range(5):
                padded_y = 2 * pair + lane
                sy = -1 if padded_y == 0 else 1 if padded_y == 9 else 0
                y = (padded_y - 1) % 8
                mid, low, high = (source[slots[sy, sz], pl.ds(x_from, count), y] for sz in (0, -1, 1))
                tiles.append((
                    pltpu.roll(jnp.where(row == 7, low, mid), 1, 1),
                    mid,
                    pltpu.roll(jnp.where(row == 0, high, mid), 7, 1),
                ))
            for shift in range(3):
                for q in range(2):
                    for half in range(2):
                        both = jnp.concatenate([tiles[q + 2 * half][shift], tiles[q + 2 * half + 1][shift]], axis=1)
                        pads[shift, q, b, pl.ds(x_to, count), half * 16:(half + 1) * 16, lane * C:(lane + 1) * C] = both.astype(BF16)

    def assemble_own(i, carry):
        x = (i % 4) * 2
        assemble(i // 4, grads, 1, x, 2, x + 1)
        return carry

    lax.fori_loop(0, SLOTS * 4, assemble_own, 0)

    arrive(gather_z)
    here = rows.at[core, c1, c2]
    gather_2 = go([remote(here, here, g2_sems, t, peer2(t)) for t in range(1, 4)])

    def window(step_x, step_z, q, bricks):
        found = pads[2 - step_z, q, bricks, pl.ds(2 - step_x, 8), :, :]
        return found.reshape(found.shape[0] * 256, 256)

    def filter_terms(step_x, step_z, carry):
        left = acts_t[...]
        q0, q1 = (
            jnp.dot(left, window(step_x, step_z, q, pl.ds(0, SLOTS)), preferred_element_type=F32) for q in range(2)
        )
        for step_y, term in (
            (0, q1[:C, :C] + q1[C:, C:]),
            (1, q0[:C, C:] + q1[C:, :C]),
            (2, q0[:C, :C] + q0[C:, C:]),
        ):
            tap = step_x * 9 + step_y * 3 + step_z
            filt_sum[pl.ds(pl.multiple_of(tap * C, C), C), :] = term
        return carry

    lax.fori_loop(0, 3, lambda step_z, carry: filter_terms(1, step_z, carry), 0)

    arrive(gather_2)
    here = rows.at[core, c1]
    gather_1 = go([remote(here, here, g1_sems, t, peer1(t)) for t in range(1, 4)])

    arrive(halos)

    def widen(b, carry):
        for side in range(2):
            halo[side, b] = halo_in[side, b].astype(F32).reshape(1, 8, 8, C)
        return carry

    lax.fori_loop(0, SLOTS, widen, 0)

    def assemble_halo(b, carry):
        assemble(b, halo.at[0], 0, 0, 1, 0)
        assemble(b, halo.at[1], 2, 0, 1, 9)
        return carry

    lax.fori_loop(0, SLOTS, assemble_halo, 0)
    lax.fori_loop(0, 3, lambda step_z, carry: filter_terms(0, step_z, carry), 0)

    arrive(gather_1)
    here = rows.at[core]
    gather_last = go([remote(here, here, gp_sems, 0, partner)])

    lax.fori_loop(0, 3, lambda step_z, carry: filter_terms(2, step_z, carry), 0)

    def deal(i, carry):
        block = filt_sum.at[pl.ds(pl.multiple_of(i * 216, 8), 224)]
        for k in range(8):
            rs_pair[0, i // 4, i % 4, k] = block[27 * k:27 * k + 16]
            rs_pair[1, i % 4, i // 4, k] = block[27 * k + 16:27 * k + 32]
        return carry

    lax.fori_loop(0, 16, deal, 0)
    reduce_pair = go([remote(rs_pair.at[1 - core], rs_pair_in, rp_sems, 0, partner)])

    arrive(gather_last)

    def undeal(i, carry):
        block = filt_full.at[pl.ds(pl.multiple_of(i * 216, 8), 224)]
        for k in range(8):
            block[27 * k:27 * k + 16] = rows[0, i // 4, i % 4, k].astype(F32)
            block[27 * k + 16:27 * k + 32] = rows[1, i % 4, i // 4, k].astype(F32)
        return carry

    lax.fori_loop(0, 16, undeal, 0)

    def build_weights(i, carry):
        step_x, step_z = i // 3, i % 3
        taps = []
        for step_y in range(3):
            tap = step_x * 9 + step_y * 3 + step_z
            taps.append(filt_full[pl.ds(pl.multiple_of(tap * C, C), C), :].T.astype(BF16))
        zero = jnp.zeros((C, C), BF16)
        for q in range(2):
            for lane in range(2):
                for parity in range(2):
                    step_y = parity - (2 * q + lane - 1) + 1
                    block = taps[step_y] if 0 <= step_y <= 2 else zero
                    weights[i, q * 256 + lane * C:q * 256 + (lane + 1) * C, parity * C:(parity + 1) * C] = block
        return carry

    lax.fori_loop(0, 9, build_weights, 0)

    def input_terms(i, carry):
        total = None
        for step in range(9):
            for q in range(2):
                term = jnp.dot(
                    window(step // 3, step % 3, q, pl.ds(i * 2, 2)),
                    weights[step, q * 256:(q + 1) * 256, :],
                    preferred_element_type=F32,
                )
                total = term if total is None else total + term
        total = total.reshape(64, 8, 2 * C)
        both = jnp.stack([total[:, :, :C], total[:, :, C:]], axis=1)
        in_grad[pl.ds(i * 2, 2)] = both.reshape(2, VOX, C).astype(BF16)
        return carry

    stores = []

    def input_segment(part):
        lax.fori_loop(part * 2, part * 2 + 2, input_terms, 0)
        span = pl.ds(part * 4, 4)
        item = pltpu.make_async_copy(in_grad.at[span], in_grad_hbm.at[span], store_sem.at[part])
        item.start()
        stores.append(item)

    input_segment(0)

    arrive(reduce_pair)

    def add_pair(i, carry):
        total = rs_pair[core, i // 4, i % 4] + rs_pair_in[i // 4, i % 4]
        sum1[i // 4, i % 4] = total
        send1[i // 4, i % 4] = total.astype(BF16)
        return carry

    lax.fori_loop(0, 16, add_pair, 0)
    reduce_1 = go([remote(send1.at[(c1 + t) % 4], recv1.at[t - 1], r1_sems, t, peer1(t)) for t in range(1, 4)])

    input_segment(1)

    arrive(reduce_1)

    def add_1(i, carry):
        total = sum1[c1, i]
        for t in range(3):
            total = total + recv1[t, i].astype(F32)
        sum2[i] = total
        send2[i] = total.astype(BF16)
        return carry

    lax.fori_loop(0, 4, add_1, 0)
    reduce_2 = go([remote(send2.at[(c2 + t) % 4], recv2.at[t - 1], r2_sems, t, peer2(t)) for t in range(1, 4)])

    input_segment(2)

    arrive(reduce_2)
    total = sum2[c2]
    for t in range(3):
        total = total + recv2[t].astype(F32)
    sum2[0] = total
    send3[...] = total.astype(BF16)
    reduce_z = go([remote(send3.at[(z + t) % 8], recv3.at[t - 1], r3_sems, t, peerz(t)) for t in range(1, 8)])
    arrive(reduce_z)
    total = sum2[0, z]
    for t in range(7):
        total = total + recv3[t].astype(F32)
    sum4[...] = total
    reduce_last = go([remote(sum4, recv4, r4_sems, 0, partner)])
    arrive(reduce_last)
    scale = 1.0 / math.sqrt(BRICKS * VOX)
    mine, other = sum4[...], recv4[...]
    both = jnp.concatenate([jnp.where(core == 0, mine, other), jnp.where(core == 0, other, mine)], axis=0) * scale
    both = jnp.where(core == 0, both, pltpu.roll(both, 64, 1))
    filt_grad_ref[...] = both[0:27, 0:64]
    for item in stores:
        item.wait()
    for item in started:
        item.wait_send()


def on_device(acts, preact, cotangent, filt, counts, neighbors):
    vmem, dma = pltpu.VMEM, pltpu.SemaphoreType.DMA
    any_space = pl.BlockSpec(memory_space=pl.ANY)
    in_smem = pl.BlockSpec(memory_space=pltpu.SMEM)
    in_vmem = pl.BlockSpec(memory_space=pltpu.VMEM)
    return pl.pallas_call(
        kernel,
        out_shape=(
            jax.ShapeDtypeStruct((SLOTS, VOX, C), BF16),
            jax.ShapeDtypeStruct((27, 64), F32),
        ),
        in_specs=[in_smem, in_smem, any_space, any_space, any_space, in_vmem],
        out_specs=(any_space, in_vmem),
        scratch_shapes=[
            vmem((SLOTS, VOX, C), BF16),
            vmem((SLOTS, VOX, C), BF16),
            vmem((SLOTS, VOX, C), BF16),
            vmem((SLOTS + 1, 8, 8, 8, C), F32),
            vmem((2, SLOTS, 64, C), BF16),
            vmem((2, SLOTS, 64, C), BF16),
            vmem((2, SLOTS + 1, 1, 8, 8, C), F32),
            vmem((3, 2, SLOTS, 10, 32, 2 * C), BF16),
            vmem((2 * C, SLOTS * 256), BF16),
            vmem((9, 512, 256), BF16),
            vmem((3464, C), F32),
            vmem((3464, C), F32),
            vmem((32, C), BF16),
            vmem((32, C), BF16),
            vmem((2, 4, 4, 8, 16, C), BF16),
            vmem((2, 4, 4, 8, 16, C), F32),
            vmem((4, 4, 8, 16, C), F32),
            vmem((4, 4, 8, 16, C), F32),
            vmem((4, 4, 8, 16, C), BF16),
            vmem((3, 4, 8, 16, C), BF16),
            vmem((4, 8, 16, C), F32),
            vmem((4, 8, 16, C), BF16),
            vmem((3, 8, 16, C), BF16),
            vmem((8, 16, C), BF16),
            vmem((7, 16, C), BF16),
            vmem((16, C), F32),
            vmem((16, C), F32),
            vmem((SLOTS, VOX, C), BF16),
            dma((9,)), dma((SEGMENTS,)),
            dma((2, 2)), dma((2, 1)), dma((2, 8)), dma((2, 4)), dma((2, 4)), dma((2, 1)),
            dma((2, 1)), dma((2, 4)), dma((2, 4)), dma((2, 8)), dma((2, 1)),
        ],
        compiler_params=pltpu.CompilerParams(
            collective_id=0, has_side_effects=True, vmem_limit_bytes=62_000_000
        ),
        name="brick_backward",
    )(counts, neighbors, acts, preact, cotangent, filt)


def solution(mesh):
    in_specs = (
        P(("space", "rep"), None, None),
        P(("space", "rep"), None, None),
        P(("space", "rep"), None, None),
        P("space", "rep"),
        P(),
        P(("space", "rep"), None),
    )
    out_specs = (P(("space", "rep"), None, None), P("space", "rep"))
    return jax.shard_map(
        on_device, mesh=mesh, in_specs=in_specs, out_specs=out_specs, check_vma=False
    )
```

time: 1390 us -> 57.7 us (0.04)
  blocking collectives: 651 us -> 0 us
  local copies, waits for them, and re-layouts: 392 us -> 3.27 us
  other arithmetic: 94.9 us -> 0 us
  starting transfers between devices: 92.6 us -> 0 us
  matrix products: 71.2 us -> 0 us
  waiting for transfers between devices: 70.8 us -> 0 us
  Pallas kernels: 0 us -> 53.7 us
  between operations: 15.7 us -> 0.65 us
    all_gather x2 -> x0, blocking collectives: 354 us -> none  [the longest x1 295 us: on_device(): gathered_rows = lax.all_gather(filt, 'space', axis=0, tiled=True)]
    unnamed x1 -> x0, blocking collectives: 297 us -> none
    while x672 -> x0, local copies, waits for them, and re-layouts: 256 us -> none
    gather x54 -> x0, local copies, waits for them, and re-layouts: 97.3 us -> none  [assemble(): fetched = jnp.take(source, indices[:, tap], axis=0)]
    unnamed x21 -> x0, starting transfers between devices: 80 us -> none
    dot_general x24 -> x0, matrix products: 71.2 us -> none  [the longest x12 50.3 us: per_brick(): lax.dot_general(unrolled_act, center, (((0,), (0,)), ((), ())), preferred...]
    unnamed x22 -> x0, waiting for transfers between devices: 70.8 us -> none
    pallas_call x0 -> x1, Pallas kernels: none -> 53.7 us  [on_device(): pl.pallas_call(kernel, out_shape=(jax.ShapeDtypeStruct((SLOTS, VOX, C), B...]
  transfers between devices with their start and end apart: 25 -> 0, of which waited for: 2 -> 0; matrix products, arithmetic and copies ran while one was open for 10% -> 0% of each run, Pallas kernels for 0% -> 0%
where the time goes in v1:
time: 57.7 us; the launch traced here: 57.6 us
  Pallas kernels  53.7 us (93%)
  local copies, waits for them, and re-layouts  3.27 us (6%)
  between operations  0.65 us (1%)
    pallas_call x1, Pallas kernels, on_device(): pl.pallas_call(kernel, out_shape=(jax.ShapeDtypeStruct((SLOTS, VOX, C), B...  53.7 us
    unnamed x4, local copies, waits for them, and re-layouts  3.27 us

profile of v1, /device:TPU:1, one launch (start us, length us, event | category | flops | bytes accessed | tf_op | source)
XLA Modules:
  0.0 57.6 jit_solution(2201959924984186551)
XLA Ops:
  0.6 53.7 %brick_backward.1 = (bf16[12,512,128]{2,1,0:T(8,128)(2,1)}, f32[27,64]{1,0:T(8,128)}) custom-call(s32[256]{0:T(256)} %counts.1, s32[12,27]{1,0:T(8,128)} %neighbors.1, bf16[12,512,128]{2,1,0:T(8,128)(2,1)} %acts_hbm.1, bf16[12,512,128]{2,1,0:T(8,128)(2,1)} %pre_hbm.1, bf16[12,512,128]{2,1,0:T(8,128)(2,1)} %cot_hbm.1, bf16[27,64]{1,0:T(8,128)(2,1)} %filt_ref.1), custom_call_target="tpu_custom_call" | custom-call | tf_op jit(solution)/shard_map/brick_backward/pallas_call | solution.py:356
  54.3 0.0 copy-start
  54.3 2.7 %copy.10 = bf16[12,512,128]{2,1,0:T(8,128)(2,1)} copy(bf16[12,512,128]{2,1,0:T(8,128)(2,1)} %get-tuple-element.4) | data formatting | bytes 3145728
  57.0 0.0 copy-done
  57.0 0.6 %copy.11 = f32[27,64]{1,0:T(8,128)} copy(f32[27,64]{1,0:T(8,128)S(1)} %copy-done) | data formatting | bytes 13824
Async XLA Ops:
  54.3 2.7 %copy-start = (f32[27,64]{1,0:T(8,128)S(1)}, f32[27,64]{1,0:T(8,128)}, u32[]{:S(2)}) copy-start(f32[27,64]{1,0:T(8,128)} %get-tuple-element.5) | copy-start | bytes 20740

commit v2 on v1

v2 whole, which is shorter than its diff:
```python
import math

import jax
import jax.numpy as jnp
from jax import lax
from jax.experimental import pallas as pl
from jax.experimental.pallas import tpu as pltpu
from jax.sharding import PartitionSpec as P


SLOTS = 12
VOX = 512
C = 128
DEVICES = 256
CHIPS = 128
BRICKS = SLOTS * DEVICES
F32 = jnp.float32
BF16 = jnp.bfloat16
MESH = pl.DeviceIdType.MESH
ITEMS = 8


def slope_times(cotangent, preact):
    values = preact.astype(F32)
    sigma = 0.5 + 0.5 * jnp.tanh(0.5 * values)
    return cotangent.astype(F32) * (sigma * (1.0 + values * (1.0 - sigma)))


def kernel(
    counts, neighbors, neighbors_vmem, acts_hbm, pre_hbm, cot_hbm, filt_ref, in_grad_hbm, filt_grad_ref,
    acts, pre, cot, grads, own_g, other_g, halo_out, halo_in, table_in, table, pads, acts_t, weights,
    filt_sum, filt_full, rows, rs_pair, rs_pair_in, sum1, send1, recv1, send2, recv2, in_grad, returned,
    load_sem, store_sem, table_sem, pair_sems, halo_sems, gz_sems, gxy_sems, gp_sems, rp_sems, rxy_sems, rz_sems,
):
    chip = lax.axis_index("space")
    core = lax.axis_index("rep")
    device = chip * 2 + core
    z = chip % 8
    xy = chip // 8

    def to(chip_id, core_id):
        return {"space": chip_id, "rep": core_id}

    partner = to(chip, 1 - core)
    next_chip = (chip + 1) % CHIPS
    last_chip = (chip + CHIPS - 1) % CHIPS

    def peer_xy(t):
        return to((xy + t) % 16 * 8 + z, core)

    def peer_z(t):
        return to(xy * 8 + (z + t) % 8, core)

    def load(source, target, part, index):
        span = pl.ds(part * 4, 4)
        return pltpu.make_async_copy(source.at[span], target.at[span], load_sem.at[index * 3 + part])

    pairs = ((pre_hbm, pre), (cot_hbm, cot), (acts_hbm, acts))
    loads = [load(s, t, part, i) for i, (s, t) in enumerate(pairs) for part in range(3)]
    for item in loads:
        item.start()

    barrier = pltpu.get_barrier_semaphore()
    greeted = [partner, to(next_chip, 0), to(last_chip, 1)]
    greeted += [peer_z(t) for t in range(1, 8)] + [peer_xy(t) for t in range(1, 16)]
    for other in greeted:
        pl.semaphore_signal(barrier, inc=1, device_id=other, device_id_type=MESH)

    def remote(source, target, sems, index, other, landing=None):
        return pltpu.make_async_remote_copy(
            src_ref=source, dst_ref=target, send_sem=sems.at[0, index],
            recv_sem=sems.at[1, index if landing is None else landing],
            device_id=other, device_id_type=MESH,
        )

    started = []

    def go(copies):
        for item in copies:
            item.start()
        started.extend(copies)
        return copies

    def arrive(copies):
        for item in copies:
            item.wait_recv()

    left = lax.broadcasted_iota(jnp.int32, (1, C), 1) < 64

    def swap(top, bottom):
        return jnp.where(left, top, pltpu.roll(bottom, 64, 1)), jnp.where(left, pltpu.roll(top, 64, 1), bottom)

    filt_sum[0:32, :] = jnp.zeros((32, C), F32)
    filt_sum[0:27, 0:64] = filt_ref[...].astype(F32)
    rows[core, xy, z] = swap(filt_sum[0:16, :], filt_sum[16:32, :])[0].astype(BF16)
    filt_sum[3456:3464, :] = jnp.zeros((8, C), F32)
    empty = jnp.zeros((8, 8, C), F32)
    grads[0, SLOTS, 7] = empty
    grads[3, SLOTS, 0] = empty
    for x in range(8):
        grads[1, SLOTS, x] = empty
        grads[2, SLOTS, x] = empty

    own_count = counts[device]
    other_count = counts[device + 1 - 2 * core]
    for item in loads[:6]:
        item.wait()

    def outer_layer(b, carry):
        span = pl.ds(pl.multiple_of(core * 448, 64), 64)
        g = slope_times(cot[b, span, :], pre[b, span, :])
        grads[1 + core, b, 7 * core] = g.reshape(8, 8, C)
        halo_out[b] = g.astype(BF16)
        own_g[b, span, :] = g.astype(BF16)
        return carry

    lax.fori_loop(0, SLOTS, outer_layer, 0)
    pl.semaphore_wait(barrier, len(greeted))
    facing = (chip + CHIPS - 1 + 2 * core) % CHIPS
    go([remote(halo_out, halo_in.at[1 - core], halo_sems, side, to(facing, side), 1 - core) for side in range(2)])
    swap_table = go([remote(neighbors_vmem, table_in, pair_sems, 0, partner)])
    swap_acts = go([remote(acts_hbm.at[pl.ds(8, 4)], acts.at[pl.ds(SLOTS, 4)], pair_sems, 1, partner)])
    here = rows.at[core, xy, z]
    gather_z = go([remote(here, here, gz_sems, t, peer_z(t)) for t in range(1, 8)])

    def inner_layers(b, carry):
        for j in range(7):
            x = j + 1 - core
            span = pl.ds(pl.multiple_of(x * 64, 64), 64)
            g = slope_times(cot[b, span, :], pre[b, span, :])
            grads[1 + core, b, x] = g.reshape(8, 8, C)
            own_g[b, span, :] = g.astype(BF16)
        return carry

    lax.fori_loop(0, SLOTS, inner_layers, 0)
    swap_g = go([remote(own_g, other_g, pair_sems, 2, partner)])
    arrive(swap_table)
    table_copy = pltpu.make_async_copy(table_in, table, table_sem)
    table_copy.start()
    for item in loads[6:]:
        item.wait()
    arrive(swap_acts)

    def foreign(i):
        return (i >= 4) & (15 - i < other_count)

    def transpose_acts(i, carry):
        brick = jnp.where(foreign(i), SLOTS + 7 - i, i)
        a = acts[brick].astype(F32).reshape(32, 2, 8, C)
        span = pl.ds(pl.multiple_of(i * 256, 256), 256)
        for parity in range(2):
            acts_t[parity * C:(parity + 1) * C, span] = a[:, parity].reshape(256, C).T.astype(BF16)
        return carry

    lax.fori_loop(0, ITEMS, transpose_acts, 0)
    table_copy.wait()

    row = lax.broadcasted_iota(jnp.int32, (1, 8, C), 1)

    def assemble(i, layer, planes):
        taken = foreign(i)
        live = taken | (i < own_count)
        parity = jnp.where(taken, 1 - core, core)
        first = (chip * 2 + parity + layer - 1) * SLOTS
        mirror = jnp.where(i >= 4, 15 - i, i)

        def slot(step_y, step_z):
            tap = layer * 9 + (step_y + 1) * 3 + step_z + 1
            index = jnp.where(taken, table[mirror, tap], neighbors[i, tap])
            return jnp.where((index < BRICKS) & live, jnp.clip(index - first, 0, SLOTS - 1), SLOTS)

        slots = {(sy, sz): slot(sy, sz) for sy in (-1, 0, 1) for sz in (-1, 0, 1)}
        for x_from, count, x_to in planes:
            for lane in range(2):
                tiles = []
                for pair in range(5):
                    padded_y = 2 * pair + lane
                    sy = -1 if padded_y == 0 else 1 if padded_y == 9 else 0
                    y = (padded_y - 1) % 8
                    mid, low, high = (
                        grads[parity + layer, slots[sy, sz], x_from:x_from + count, y] for sz in (0, -1, 1)
                    )
                    tiles.append((
                        pltpu.roll(jnp.where(row == 7, low, mid), 1, 1),
                        mid,
                        pltpu.roll(jnp.where(row == 0, high, mid), 7, 1),
                    ))
                for shift in range(3):
                    for q in range(2):
                        for half in range(2):
                            both = jnp.concatenate(
                                [tiles[q + 2 * half][shift], tiles[q + 2 * half + 1][shift]], axis=1
                            )
                            pads[
                                shift, q, i, x_to:x_to + count, half * 16:(half + 1) * 16, lane * C:(lane + 1) * C
                            ] = both.astype(BF16)

    def assemble_own(i, carry):
        assemble(i, 1, [(x, 2, x + 1) for x in range(0, 8, 2)])
        return carry

    lax.fori_loop(0, 4, assemble_own, 0)
    arrive(gather_z)
    here = rows.at[core, xy]
    gather_xy = go([remote(here, here, gxy_sems, t, peer_xy(t)) for t in range(1, 16)])
    arrive(swap_g)

    def widen(b, carry):
        grads[2 - core, b] = other_g[b].astype(F32).reshape(8, 8, 8, C)
        return carry

    lax.fori_loop(0, SLOTS, widen, 0)
    lax.fori_loop(4, ITEMS, assemble_own, 0)

    def window(step_x, step_z, q, items):
        found = pads[2 - step_z, q, items, pl.ds(2 - step_x, 8), :, :]
        return found.reshape(found.shape[0] * 256, 256)

    def filter_terms(step_x, step_z, carry):
        lhs = acts_t[...]
        q0, q1 = (
            jnp.dot(lhs, window(step_x, step_z, q, pl.ds(0, ITEMS)), preferred_element_type=F32) for q in range(2)
        )
        for step_y, term in (
            (0, q1[:C, :C] + q1[C:, C:]),
            (1, q0[:C, C:] + q1[C:, :C]),
            (2, q0[:C, :C] + q0[C:, C:]),
        ):
            tap = step_x * 9 + step_y * 3 + step_z
            filt_sum[pl.ds(pl.multiple_of(tap * C, C), C), :] = term
        return carry

    lax.fori_loop(0, 3, lambda step_z, carry: filter_terms(1, step_z, carry), 0)

    for side in range(2):
        remote(halo_out, halo_in.at[side], halo_sems, 0, partner, side).wait_recv()

    def widen_halo(b, carry):
        grads[0, b, 7] = halo_in[0, b].astype(F32).reshape(8, 8, C)
        grads[3, b, 0] = halo_in[1, b].astype(F32).reshape(8, 8, C)
        return carry

    lax.fori_loop(0, SLOTS, widen_halo, 0)

    def assemble_halo(i, carry):
        assemble(i, 0, [(7, 1, 0)])
        assemble(i, 2, [(0, 1, 9)])
        return carry

    lax.fori_loop(0, ITEMS, assemble_halo, 0)
    lax.fori_loop(0, 3, lambda step_z, carry: filter_terms(0, step_z, carry), 0)

    def deal(i, carry):
        block = filt_sum.at[pl.ds(pl.multiple_of(i * 216, 8), 224)]
        for k in range(8):
            rs_pair[0, i, k], rs_pair[1, i, k] = swap(block[27 * k:27 * k + 16], block[27 * k + 16:27 * k + 32])
        return carry

    def pair_half(part):
        span = pl.ds(part * 8, 8)
        return go([remote(rs_pair.at[1 - core, span], rs_pair_in.at[span], rp_sems, part, partner)])

    def add_pair(i, carry):
        total = rs_pair[core, i] + rs_pair_in[i]
        sum1[i] = total
        send1[i] = total.astype(BF16)
        return carry

    def send_half(part):
        for target in range(part * 8, part * 8 + 8):
            @pl.when(target != xy)
            def _():
                remote(send1.at[target], recv1.at[xy], rxy_sems, target, to(target * 8 + z, core), xy).start()

    lax.fori_loop(0, 8, deal, 0)
    reduce_pair = pair_half(0)
    arrive(gather_xy)
    here = rows.at[core]
    gather_last = go([remote(here, here, gp_sems, 0, partner)])
    lax.fori_loop(0, 2, lambda step_z, carry: filter_terms(2, step_z, carry), 0)
    arrive(reduce_pair)
    lax.fori_loop(0, 8, add_pair, 0)
    send_half(0)
    lax.fori_loop(2, 3, lambda step_z, carry: filter_terms(2, step_z, carry), 0)
    lax.fori_loop(8, 16, deal, 0)
    reduce_pair = pair_half(1)

    arrive(gather_last)

    def undeal(i, carry):
        block = filt_full.at[pl.ds(pl.multiple_of(i * 216, 8), 224)]
        for k in range(8):
            top, bottom = swap(rows[0, i, k].astype(F32), rows[1, i, k].astype(F32))
            block[27 * k:27 * k + 16] = top
            block[27 * k + 16:27 * k + 32] = bottom
        return carry

    lax.fori_loop(0, 16, undeal, 0)
    arrive(reduce_pair)
    lax.fori_loop(8, 16, add_pair, 0)
    send_half(1)

    def build_weights(i, carry):
        step_x, step_z = i // 3, i % 3
        taps = []
        for step_y in range(3):
            tap = step_x * 9 + step_y * 3 + step_z
            taps.append(filt_full[pl.ds(pl.multiple_of(tap * C, C), C), :].T.astype(BF16))
        zero = jnp.zeros((C, C), BF16)
        for q in range(2):
            for lane in range(2):
                for parity in range(2):
                    step_y = parity - (2 * q + lane - 1) + 1
                    block = taps[step_y] if 0 <= step_y <= 2 else zero
                    weights[i, q * 256 + lane * C:q * 256 + (lane + 1) * C, parity * C:(parity + 1) * C] = block
        return carry

    lax.fori_loop(0, 9, build_weights, 0)

    def input_terms(pair):
        total = None
        for step in range(9):
            for q in range(2):
                term = jnp.dot(
                    window(step // 3, step % 3, q, pl.ds(pair * 2, 2)),
                    weights[step, q * 256:(q + 1) * 256, :],
                    preferred_element_type=F32,
                )
                total = term if total is None else total + term
        total = total.reshape(64, 8, 2 * C)
        both = jnp.stack([total[:, :, :C], total[:, :, C:]], axis=1)
        return both.reshape(2, VOX, C)

    stores = []

    def store(part):
        span = pl.ds(part * 4, 4)
        item = pltpu.make_async_copy(in_grad.at[span], in_grad_hbm.at[span], store_sem.at[part])
        item.start()
        stores.append(item)

    def upper_items(pair, carry):
        found = input_terms(pair)
        for k in range(2):
            i = pair * 2 + k
            taken = foreign(i)
            in_grad[i] = jnp.where(taken, 0.0, found[k]).astype(BF16)
            returned[7 - i] = jnp.where(taken, found[k], 0.0).astype(BF16)
        return carry

    lax.fori_loop(2, 4, upper_items, 0)
    give_back = go([remote(returned, in_grad.at[pl.ds(8, 4)], pair_sems, 3, partner)])
    store(1)

    def lower_items(pair, carry):
        in_grad[pl.ds(pair * 2, 2)] = input_terms(pair).astype(BF16)
        return carry

    lax.fori_loop(0, 2, lower_items, 0)
    store(0)
    arrive(give_back)
    store(2)

    for source in range(16):
        @pl.when(source != xy)
        def _():
            remote(send1.at[source], recv1.at[source], rxy_sems, source, partner).wait_recv()
    recv1[xy] = jnp.zeros((8, 16, C), BF16)
    total = sum1[xy]
    for t in range(16):
        total = total + recv1[t].astype(F32)
    sum1[xy] = total
    send2[...] = total.astype(BF16)
    reduce_z = go([remote(send2.at[(z + t) % 8], recv2.at[t - 1], rz_sems, t, peer_z(t)) for t in range(1, 8)])
    arrive(reduce_z)
    total = sum1[xy, z]
    for t in range(7):
        total = total + recv2[t].astype(F32)
    total = total * (1.0 / math.sqrt(BRICKS * VOX))
    filt_grad_ref[0:16, :] = total[:, 0:64]
    filt_grad_ref[16:27, :] = total[0:11, 64:128]
    for item in stores:
        item.wait()
    for item in started:
        item.wait_send()
    for target in range(16):
        @pl.when(target != xy)
        def _():
            remote(send1.at[target], recv1.at[target], rxy_sems, target, partner).wait_send()


def hand_over(source, filt_ref, target, filt_out, buffer, in_sem, out_sem):
    parts = [pl.ds(k * 4, 4) for k in range(3)]
    reads = [pltpu.make_async_copy(source.at[p], buffer.at[p], in_sem.at[k]) for k, p in enumerate(parts)]
    writes = [pltpu.make_async_copy(buffer.at[p], target.at[p], out_sem.at[k]) for k, p in enumerate(parts)]
    for item in reads:
        item.start()
    filt_out[...] = filt_ref[...]
    for k in range(3):
        reads[k].wait()
        writes[k].start()
    for item in writes:
        item.wait()


def on_device(acts, preact, cotangent, filt, counts, neighbors):
    vmem, dma = pltpu.VMEM, pltpu.SemaphoreType.DMA
    any_space = pl.BlockSpec(memory_space=pl.ANY)
    in_smem = pl.BlockSpec(memory_space=pltpu.SMEM)
    in_vmem = pl.BlockSpec(memory_space=pltpu.VMEM)
    out_shape = (
        jax.ShapeDtypeStruct((SLOTS, VOX, C), BF16),
        jax.ShapeDtypeStruct((27, 64), F32),
    )
    found = pl.pallas_call(
        kernel,
        out_shape=out_shape,
        in_specs=[in_smem, in_smem, in_vmem, any_space, any_space, any_space, in_vmem],
        out_specs=(any_space, in_vmem),
        scratch_shapes=[
            vmem((SLOTS + 4, VOX, C), BF16),
            vmem((SLOTS, VOX, C), BF16),
            vmem((SLOTS, VOX, C), BF16),
            vmem((4, SLOTS + 1, 8, 8, 8, C), F32),
            vmem((SLOTS, VOX, C), BF16),
            vmem((SLOTS, VOX, C), BF16),
            vmem((SLOTS, 64, C), BF16),
            vmem((2, SLOTS, 64, C), BF16),
            vmem((SLOTS, 27), jnp.int32),
            pltpu.SMEM((SLOTS, 27), jnp.int32),
            vmem((3, 2, ITEMS, 10, 32, 2 * C), BF16),
            vmem((2 * C, ITEMS * 256), BF16),
            vmem((9, 512, 256), BF16),
            vmem((3464, C), F32),
            vmem((3464, C), F32),
            vmem((2, 16, 8, 16, C), BF16),
            vmem((2, 16, 8, 16, C), F32),
            vmem((16, 8, 16, C), F32),
            vmem((16, 8, 16, C), F32),
            vmem((16, 8, 16, C), BF16),
            vmem((16, 8, 16, C), BF16),
            vmem((8, 16, C), BF16),
            vmem((7, 16, C), BF16),
            vmem((SLOTS, VOX, C), BF16),
            vmem((4, VOX, C), BF16),
            dma((9,)), dma((3,)), dma(()), dma((2, 4)), dma((2, 2)), dma((2, 8)), dma((2, 16)), dma((2, 1)),
            dma((2, 2)), dma((2, 16)), dma((2, 8)),
        ],
        compiler_params=pltpu.CompilerParams(
            collective_id=0, has_side_effects=True, vmem_limit_bytes=62_000_000
        ),
        name="brick_backward",
    )(counts, neighbors, neighbors, acts, preact, cotangent, filt)
    return pl.pallas_call(
        hand_over,
        out_shape=out_shape,
        in_specs=[any_space, in_vmem],
        out_specs=(any_space, in_vmem),
        scratch_shapes=[vmem((SLOTS, VOX, C), BF16), dma((3,)), dma((3,))],
        name="hand_over",
    )(*found)


def solution(mesh):
    in_specs = (
        P(("space", "rep"), None, None),
        P(("space", "rep"), None, None),
        P(("space", "rep"), None, None),
        P("space", "rep"),
        P(),
        P(("space", "rep"), None),
    )
    out_specs = (P(("space", "rep"), None, None), P("space", "rep"))
    return jax.shard_map(
        on_device, mesh=mesh, in_specs=in_specs, out_specs=out_specs, check_vma=False
    )
```

time: 57.7 us -> 50.2 us (0.87)
  Pallas kernels: 53.7 us -> 49.1 us
  local copies, waits for them, and re-layouts: 3.27 us -> 0 us
    pallas_call x1 -> x2, Pallas kernels: 53.7 us -> 49.1 us  [the longest x1 45.5 us: on_device(): pl.pallas_call(kernel, out_shape=out_shape, in_specs=[in_smem, in_smem, i...]
    unnamed x4 -> x0, local copies, waits for them, and re-layouts: 3.27 us -> none
where the time goes in v2:
time: 50.2 us; the launch traced here: 49.7 us
  Pallas kernels  49.1 us (98%)
  between operations  0.64 us (1%)
    pallas_call x1, Pallas kernels, on_device(): pl.pallas_call(kernel, out_shape=out_shape, in_specs=[in_smem, in_smem, i...  45.5 us
    pallas_call x1, Pallas kernels, on_device(): pl.pallas_call(hand_over, out_shape=out_shape, in_specs=[any_space, in_vm...  3.55 us

profile of v2, /device:TPU:1, one launch (start us, length us, event | category | flops | bytes accessed | tf_op | source)
XLA Modules:
  0.0 49.7 jit_solution(869566452474999216)
XLA Ops:
  0.6 45.5 %brick_backward.1 = (bf16[12,512,128]{2,1,0:T(8,128)(2,1)}, f32[27,64]{1,0:T(8,128)}) custom-call(s32[256]{0:T(256)} %counts.1, s32[12,27]{1,0:T(8,128)} %neighbors_vmem.1, s32[12,27]{1,0:T(8,128)} %neighbors_vmem.1, bf16[12,512,128]{2,1,0:T(8,128)(2,1)} %acts_hbm.1, bf16[12,512,128]{2,1,0:T(8,128)(2,1)} %pre_hbm.1, bf16[12,512,128]{2,1,0:T(8,128)(2,1)} %cot_hbm.1, ...), custom_call_target="tpu_custom_call" | custom-call | tf_op jit(solution)/shard_map/brick_backward/pallas_call | solution.py:415
  46.2 3.6 %hand_over.1 = (bf16[12,512,128]{2,1,0:T(8,128)(2,1)}, f32[27,64]{1,0:T(8,128)}) custom-call(bf16[12,512,128]{2,1,0:T(8,128)(2,1)} %get-tuple-element.4.source, f32[27,64]{1,0:T(8,128)} %get-tuple-element.5.filt_ref), custom_call_target="tpu_custom_call" | custom-call | tf_op jit(solution)/shard_map/hand_over/pallas_call | solution.py:454

commit v3 on v2

--- a/solution.py
+++ b/solution.py
@@ -27,8 +27,8 @@
 
 
 def kernel(
-    counts, neighbors, neighbors_vmem, acts_hbm, pre_hbm, cot_hbm, filt_ref, in_grad_hbm, filt_grad_ref,
-    acts, pre, cot, grads, own_g, other_g, halo_out, halo_in, table_in, table, pads, acts_t, weights,
+    counts, neighbors, acts_hbm, pre_hbm, cot_hbm, filt_ref, in_grad_hbm, filt_grad_ref,
+    acts, pre, cot, grads, own_g, other_g, halo_out, halo_in, own_table, other_table, mixed_table, table, pads, acts_t, weights,
     filt_sum, filt_full, rows, rs_pair, rs_pair_in, sum1, send1, recv1, send2, recv2, in_grad, returned,
     load_sem, store_sem, table_sem, pair_sems, halo_sems, gz_sems, gxy_sems, gp_sems, rp_sems, rxy_sems, rz_sems,
 ):
@@ -103,6 +103,13 @@
 
     own_count = counts[device]
     other_count = counts[device + 1 - 2 * core]
+    tap = lax.broadcasted_iota(jnp.int32, (SLOTS, 27), 1)
+    brick = lax.broadcasted_iota(jnp.int32, (SLOTS, 27), 0)
+    found = neighbors[...]
+    first = (device - 1) * SLOTS + jnp.where(tap >= 9, SLOTS, 0) + jnp.where(tap >= 18, SLOTS, 0)
+    own_table[...] = jnp.where(
+        (found < BRICKS) & (brick < own_count), jnp.clip(found - first, 0, SLOTS - 1), SLOTS
+    )
     for item in loads[:6]:
         item.wait()
 
@@ -118,7 +125,7 @@
     pl.semaphore_wait(barrier, len(greeted))
     facing = (chip + CHIPS - 1 + 2 * core) % CHIPS
     go([remote(halo_out, halo_in.at[1 - core], halo_sems, side, to(facing, side), 1 - core) for side in range(2)])
-    swap_table = go([remote(neighbors_vmem, table_in, pair_sems, 0, partner)])
+    swap_table = go([remote(own_table, other_table, pair_sems, 0, partner)])
     swap_acts = go([remote(acts_hbm.at[pl.ds(8, 4)], acts.at[pl.ds(SLOTS, 4)], pair_sems, 1, partner)])
     here = rows.at[core, xy, z]
     gather_z = go([remote(here, here, gz_sems, t, peer_z(t)) for t in range(1, 8)])
@@ -132,17 +139,27 @@
             own_g[b, span, :] = g.astype(BF16)
         return carry
 
-    lax.fori_loop(0, SLOTS, inner_layers, 0)
-    swap_g = go([remote(own_g, other_g, pair_sems, 2, partner)])
-    arrive(swap_table)
-    table_copy = pltpu.make_async_copy(table_in, table, table_sem)
-    table_copy.start()
+    def foreign(i):
+        return (i >= 4) & (15 - i < other_count)
+
+    swap_g = []
+    for part in range(3):
+        lax.fori_loop(part * 4, part * 4 + 4, inner_layers, 0)
+        span = pl.ds(part * 4, 4)
+        swap_g += go([remote(own_g.at[span], other_g.at[span], pair_sems, 4 + part, partner)])
+        if part == 0:
+            arrive(swap_table)
+            mixed_table[0:4, :] = own_table[0:4, :]
+            for i in range(4, ITEMS):
+                mixed_table[i:i + 1, :] = jnp.where(foreign(i), other_table[15 - i:16 - i, :], own_table[i:i + 1, :])
+            table_copy = pltpu.make_async_copy(mixed_table, table, table_sem)
+            table_copy.start()
     for item in loads[6:]:
         item.wait()
+    arrive(gather_z)
+    here = rows.at[core, xy]
+    gather_xy = go([remote(here, here, gxy_sems, t, peer_xy(t)) for t in range(1, 16)])
     arrive(swap_acts)
-
-    def foreign(i):
-        return (i >= 4) & (15 - i < other_count)
 
     def transpose_acts(i, carry):
         brick = jnp.where(foreign(i), SLOTS + 7 - i, i)
@@ -158,18 +175,8 @@
     row = lax.broadcasted_iota(jnp.int32, (1, 8, C), 1)
 
     def assemble(i, layer, planes):
-        taken = foreign(i)
-        live = taken | (i < own_count)
-        parity = jnp.where(taken, 1 - core, core)
-        first = (chip * 2 + parity + layer - 1) * SLOTS
-        mirror = jnp.where(i >= 4, 15 - i, i)
-
-        def slot(step_y, step_z):
-            tap = layer * 9 + (step_y + 1) * 3 + step_z + 1
-            index = jnp.where(taken, table[mirror, tap], neighbors[i, tap])
-            return jnp.where((index < BRICKS) & live, jnp.clip(index - first, 0, SLOTS - 1), SLOTS)
-
-        slots = {(sy, sz): slot(sy, sz) for sy in (-1, 0, 1) for sz in (-1, 0, 1)}
+        parity = jnp.where(foreign(i), 1 - core, core)
+        slots = {(sy, sz): table[i, layer * 9 + (sy + 1) * 3 + sz + 1] for sy in (-1, 0, 1) for sz in (-1, 0, 1)}
         for x_from, count, x_to in planes:
             for lane in range(2):
                 tiles = []
@@ -200,9 +207,6 @@
         return carry
 
     lax.fori_loop(0, 4, assemble_own, 0)
-    arrive(gather_z)
-    here = rows.at[core, xy]
-    gather_xy = go([remote(here, here, gxy_sems, t, peer_xy(t)) for t in range(1, 16)])
     arrive(swap_g)
 
     def widen(b, carry):
@@ -230,34 +234,18 @@
             filt_sum[pl.ds(pl.multiple_of(tap * C, C), C), :] = term
         return carry
 
-    lax.fori_loop(0, 3, lambda step_z, carry: filter_terms(1, step_z, carry), 0)
-
-    for side in range(2):
-        remote(halo_out, halo_in.at[side], halo_sems, 0, partner, side).wait_recv()
-
-    def widen_halo(b, carry):
-        grads[0, b, 7] = halo_in[0, b].astype(F32).reshape(8, 8, C)
-        grads[3, b, 0] = halo_in[1, b].astype(F32).reshape(8, 8, C)
-        return carry
-
-    lax.fori_loop(0, SLOTS, widen_halo, 0)
-
-    def assemble_halo(i, carry):
-        assemble(i, 0, [(7, 1, 0)])
-        assemble(i, 2, [(0, 1, 9)])
-        return carry
-
-    lax.fori_loop(0, ITEMS, assemble_halo, 0)
-    lax.fori_loop(0, 3, lambda step_z, carry: filter_terms(0, step_z, carry), 0)
-
     def deal(i, carry):
         block = filt_sum.at[pl.ds(pl.multiple_of(i * 216, 8), 224)]
         for k in range(8):
             rs_pair[0, i, k], rs_pair[1, i, k] = swap(block[27 * k:27 * k + 16], block[27 * k + 16:27 * k + 32])
         return carry
 
-    def pair_half(part):
-        span = pl.ds(part * 8, 8)
+    parts = ((6, 10), (0, 6), (10, 16))
+
+    def post_pair(part):
+        low, high = parts[part]
+        lax.fori_loop(low, high, deal, 0)
+        span = pl.ds(low, high - low)
         return go([remote(rs_pair.at[1 - core, span], rs_pair_in.at[span], rp_sems, part, partner)])
 
     def add_pair(i, carry):
@@ -266,24 +254,45 @@
         send1[i] = total.astype(BF16)
         return carry
 
-    def send_half(part):
-        for target in range(part * 8, part * 8 + 8):
+    def send_on(part, reduce_pair):
+        arrive(reduce_pair)
+        low, high = parts[part]
+        lax.fori_loop(low, high, add_pair, 0)
+        for target in range(low, high):
             @pl.when(target != xy)
             def _():
                 remote(send1.at[target], recv1.at[xy], rxy_sems, target, to(target * 8 + z, core), xy).start()
 
-    lax.fori_loop(0, 8, deal, 0)
-    reduce_pair = pair_half(0)
+    lax.fori_loop(0, 3, lambda step_z, carry: filter_terms(1, step_z, carry), 0)
+    reduce_pair = post_pair(0)
+
+    for side in range(2):
+        remote(halo_out, halo_in.at[side], halo_sems, 0, partner, side).wait_recv()
+
+    def widen_halo(b, carry):
+        grads[0, b, 7] = halo_in[0, b].astype(F32).reshape(8, 8, C)
+        grads[3, b, 0] = halo_in[1, b].astype(F32).reshape(8, 8, C)
+        return carry
+
+    lax.fori_loop(0, SLOTS, widen_halo, 0)
+
+    def assemble_halo(i, carry):
+        assemble(i, 0, [(7, 1, 0)])
+        assemble(i, 2, [(0, 1, 9)])
+        return carry
+
+    lax.fori_loop(0, ITEMS, assemble_halo, 0)
+    send_on(0, reduce_pair)
+    lax.fori_loop(0, 3, lambda step_z, carry: filter_terms(0, step_z, carry), 0)
+    reduce_pair = post_pair(1)
+    lax.fori_loop(0, 1, lambda step_z, carry: filter_terms(2, step_z, carry), 0)
+    send_on(1, reduce_pair)
+    lax.fori_loop(1, 3, lambda step_z, carry: filter_terms(2, step_z, carry), 0)
+    reduce_pair = post_pair(2)
     arrive(gather_xy)
     here = rows.at[core]
     gather_last = go([remote(here, here, gp_sems, 0, partner)])
-    lax.fori_loop(0, 2, lambda step_z, carry: filter_terms(2, step_z, carry), 0)
-    arrive(reduce_pair)
-    lax.fori_loop(0, 8, add_pair, 0)
-    send_half(0)
-    lax.fori_loop(2, 3, lambda step_z, carry: filter_terms(2, step_z, carry), 0)
-    lax.fori_loop(8, 16, deal, 0)
-    reduce_pair = pair_half(1)
+    send_on(2, reduce_pair)
 
     arrive(gather_last)
 
@@ -296,9 +305,6 @@
         return carry
 
     lax.fori_loop(0, 16, undeal, 0)
-    arrive(reduce_pair)
-    lax.fori_loop(8, 16, add_pair, 0)
-    send_half(1)
 
     def build_weights(i, carry):
         step_x, step_z = i // 3, i % 3
@@ -415,7 +421,7 @@
     found = pl.pallas_call(
         kernel,
         out_shape=out_shape,
-        in_specs=[in_smem, in_smem, in_vmem, any_space, any_space, any_space, in_vmem],
+        in_specs=[in_smem, in_vmem, any_space, any_space, any_space, in_vmem],
         out_specs=(any_space, in_vmem),
         scratch_shapes=[
             vmem((SLOTS + 4, VOX, C), BF16),
@@ -427,7 +433,9 @@
             vmem((SLOTS, 64, C), BF16),
             vmem((2, SLOTS, 64, C), BF16),
             vmem((SLOTS, 27), jnp.int32),
-            pltpu.SMEM((SLOTS, 27), jnp.int32),
+            vmem((SLOTS, 27), jnp.int32),
+            vmem((ITEMS, 27), jnp.int32),
+            pltpu.SMEM((ITEMS, 27), jnp.int32),
             vmem((3, 2, ITEMS, 10, 32, 2 * C), BF16),
             vmem((2 * C, ITEMS * 256), BF16),
             vmem((9, 512, 256), BF16),
@@ -443,14 +451,14 @@
             vmem((7, 16, C), BF16),
             vmem((SLOTS, VOX, C), BF16),
             vmem((4, VOX, C), BF16),
-            dma((9,)), dma((3,)), dma(()), dma((2, 4)), dma((2, 2)), dma((2, 8)), dma((2, 16)), dma((2, 1)),
-            dma((2, 2)), dma((2, 16)), dma((2, 8)),
+            dma((9,)), dma((3,)), dma(()), dma((2, 8)), dma((2, 2)), dma((2, 8)), dma((2, 16)), dma((2, 1)),
+            dma((2, 3)), dma((2, 16)), dma((2, 8)),
         ],
         compiler_params=pltpu.CompilerParams(
             collective_id=0, has_side_effects=True, vmem_limit_bytes=62_000_000
         ),
         name="brick_backward",
-    )(counts, neighbors, neighbors, acts, preact, cotangent, filt)
+    )(counts, neighbors, acts, preact, cotangent, filt)
     return pl.pallas_call(
         hand_over,
         out_shape=out_shape,

time: 50.2 us -> 53.7 us (1.070)
  Pallas kernels: 49.1 us -> 52.8 us
    pallas_call x1, Pallas kernels: 45.5 us -> 49.2 us  [on_device(): pl.pallas_call(kernel, out_shape=out_shape, in_specs=[in_smem, in_vmem, a...]
where the time goes in v3:
time: 53.7 us; the launch traced here: 53.4 us
  Pallas kernels  52.8 us (98%)
  between operations  0.64 us (1%)
    pallas_call x1, Pallas kernels, on_device(): pl.pallas_call(kernel, out_shape=out_shape, in_specs=[in_smem, in_vmem, a...  49.2 us
    pallas_call x1, Pallas kernels, on_device(): pl.pallas_call(hand_over, out_shape=out_shape, in_specs=[any_space, in_vm...  3.55 us

profile of v3, /device:TPU:1, one launch (start us, length us, event | category | flops | bytes accessed | tf_op | source)
XLA Modules:
  0.0 53.4 jit_solution(1604760893942297664)
XLA Ops:
  0.6 49.2 %brick_backward.1 = (bf16[12,512,128]{2,1,0:T(8,128)(2,1)}, f32[27,64]{1,0:T(8,128)}) custom-call(s32[256]{0:T(256)} %counts.1, s32[12,27]{1,0:T(8,128)} %neighbors.1, bf16[12,512,128]{2,1,0:T(8,128)(2,1)} %acts_hbm.1, bf16[12,512,128]{2,1,0:T(8,128)(2,1)} %pre_hbm.1, bf16[12,512,128]{2,1,0:T(8,128)(2,1)} %cot_hbm.1, bf16[27,64]{1,0:T(8,128)(2,1)} %filt_ref.1), custom_call_target="tpu_custom_call" | custom-call | tf_op jit(solution)/shard_map/brick_backward/pallas_call | solution.py:421
  49.9 3.6 %hand_over.1 = (bf16[12,512,128]{2,1,0:T(8,128)(2,1)}, f32[27,64]{1,0:T(8,128)}) custom-call(bf16[12,512,128]{2,1,0:T(8,128)(2,1)} %get-tuple-element.4.source, f32[27,64]{1,0:T(8,128)} %get-tuple-element.5.filt_ref), custom_call_target="tpu_custom_call" | custom-call | tf_op jit(solution)/shard_map/hand_over/pallas_call | solution.py:462

commit v4 on v3

--- a/solution.py
+++ b/solution.py
@@ -123,12 +123,12 @@
 
     lax.fori_loop(0, SLOTS, outer_layer, 0)
     pl.semaphore_wait(barrier, len(greeted))
+    here = rows.at[core, xy, z]
+    gather_z = go([remote(here, here, gz_sems, t, peer_z(t)) for t in range(1, 8)])
     facing = (chip + CHIPS - 1 + 2 * core) % CHIPS
     go([remote(halo_out, halo_in.at[1 - core], halo_sems, side, to(facing, side), 1 - core) for side in range(2)])
     swap_table = go([remote(own_table, other_table, pair_sems, 0, partner)])
     swap_acts = go([remote(acts_hbm.at[pl.ds(8, 4)], acts.at[pl.ds(SLOTS, 4)], pair_sems, 1, partner)])
-    here = rows.at[core, xy, z]
-    gather_z = go([remote(here, here, gz_sems, t, peer_z(t)) for t in range(1, 8)])
 
     def inner_layers(b, carry):
         for j in range(7):
@@ -156,9 +156,6 @@
             table_copy.start()
     for item in loads[6:]:
         item.wait()
-    arrive(gather_z)
-    here = rows.at[core, xy]
-    gather_xy = go([remote(here, here, gxy_sems, t, peer_xy(t)) for t in range(1, 16)])
     arrive(swap_acts)
 
     def transpose_acts(i, carry):
@@ -263,7 +260,11 @@
             def _():
                 remote(send1.at[target], recv1.at[xy], rxy_sems, target, to(target * 8 + z, core), xy).start()
 
-    lax.fori_loop(0, 3, lambda step_z, carry: filter_terms(1, step_z, carry), 0)
+    lax.fori_loop(0, 1, lambda step_z, carry: filter_terms(1, step_z, carry), 0)
+    arrive(gather_z)
+    here = rows.at[core, xy]
+    gather_xy = go([remote(here, here, gxy_sems, t, peer_xy(t)) for t in range(1, 16)])
+    lax.fori_loop(1, 3, lambda step_z, carry: filter_terms(1, step_z, carry), 0)
     reduce_pair = post_pair(0)
 
     for side in range(2):
@@ -358,15 +359,6 @@
     give_back = go([remote(returned, in_grad.at[pl.ds(8, 4)], pair_sems, 3, partner)])
     store(1)
 
-    def lower_items(pair, carry):
-        in_grad[pl.ds(pair * 2, 2)] = input_terms(pair).astype(BF16)
-        return carry
-
-    lax.fori_loop(0, 2, lower_items, 0)
-    store(0)
-    arrive(give_back)
-    store(2)
-
     for source in range(16):
         @pl.when(source != xy)
         def _():
@@ -378,6 +370,16 @@
     sum1[xy] = total
     send2[...] = total.astype(BF16)
     reduce_z = go([remote(send2.at[(z + t) % 8], recv2.at[t - 1], rz_sems, t, peer_z(t)) for t in range(1, 8)])
+
+    def lower_items(pair, carry):
+        in_grad[pl.ds(pair * 2, 2)] = input_terms(pair).astype(BF16)
+        return carry
+
+    lax.fori_loop(0, 2, lower_items, 0)
+    store(0)
+    arrive(give_back)
+    store(2)
+
     arrive(reduce_z)
     total = sum1[xy, z]
     for t in range(7):

time: 53.7 us -> 46.3 us (0.86)
  the two profiles are of different devices: /device:TPU:1 before, /device:TPU:30 now
where the time goes in v4:
time: 46.3 us; the launch traced here: 46 us
  Pallas kernels  45.4 us (98%)
  between operations  0.64 us (1%)
    pallas_call x1, Pallas kernels, on_device(): pl.pallas_call(kernel, out_shape=out_shape, in_specs=[in_smem, in_vmem, a...  41.8 us
    pallas_call x1, Pallas kernels, on_device(): pl.pallas_call(hand_over, out_shape=out_shape, in_specs=[any_space, in_vm...  3.55 us

profile of v4, /device:TPU:30, one launch (start us, length us, event | category | flops | bytes accessed | tf_op | source)
XLA Modules:
  0.0 46.0 jit_solution(9256697022334164662)
XLA Ops:
  0.6 41.8 %brick_backward.1 = (bf16[12,512,128]{2,1,0:T(8,128)(2,1)}, f32[27,64]{1,0:T(8,128)}) custom-call(s32[256]{0:T(256)} %counts.1, s32[12,27]{1,0:T(8,128)} %neighbors.1, bf16[12,512,128]{2,1,0:T(8,128)(2,1)} %acts_hbm.1, bf16[12,512,128]{2,1,0:T(8,128)(2,1)} %pre_hbm.1, bf16[12,512,128]{2,1,0:T(8,128)(2,1)} %cot_hbm.1, bf16[27,64]{1,0:T(8,128)(2,1)} %filt_ref.1), custom_call_target="tpu_custom_call" | custom-call | tf_op jit(solution)/shard_map/brick_backward/pallas_call | solution.py:423
  42.5 3.6 %hand_over.1 = (bf16[12,512,128]{2,1,0:T(8,128)(2,1)}, f32[27,64]{1,0:T(8,128)}) custom-call(bf16[12,512,128]{2,1,0:T(8,128)(2,1)} %get-tuple-element.4.source, f32[27,64]{1,0:T(8,128)} %get-tuple-element.5.filt_ref), custom_call_target="tpu_custom_call" | custom-call | tf_op jit(solution)/shard_map/hand_over/pallas_call | solution.py:464

commit v5 on v4

--- a/solution.py
+++ b/solution.py
@@ -27,9 +27,9 @@
 
 
 def kernel(
-    counts, neighbors, acts_hbm, pre_hbm, cot_hbm, filt_ref, in_grad_hbm, filt_grad_ref,
+    counts, neighbors, acts_hbm, pre_hbm, cot_hbm, filt_ref, in_grad, filt_grad_ref,
     acts, pre, cot, grads, own_g, other_g, halo_out, halo_in, own_table, other_table, mixed_table, table, pads, acts_t, weights,
-    filt_sum, filt_full, rows, rs_pair, rs_pair_in, sum1, send1, recv1, send2, recv2, in_grad, returned,
+    filt_sum, filt_full, rows, rs_pair, rs_pair_in, sum1, send1, recv1, send2, recv2, returned, landed,
     load_sem, store_sem, table_sem, pair_sems, halo_sems, gz_sems, gxy_sems, gp_sems, rp_sems, rxy_sems, rz_sems,
 ):
     chip = lax.axis_index("space")
@@ -42,8 +42,6 @@
         return {"space": chip_id, "rep": core_id}
 
     partner = to(chip, 1 - core)
-    next_chip = (chip + 1) % CHIPS
-    last_chip = (chip + CHIPS - 1) % CHIPS
 
     def peer_xy(t):
         return to((xy + t) % 16 * 8 + z, core)
@@ -57,11 +55,12 @@
 
     pairs = ((pre_hbm, pre), (cot_hbm, cot), (acts_hbm, acts))
     loads = [load(s, t, part, i) for i, (s, t) in enumerate(pairs) for part in range(3)]
-    for item in loads:
+    for item in loads[:6]:
         item.start()
 
     barrier = pltpu.get_barrier_semaphore()
-    greeted = [partner, to(next_chip, 0), to(last_chip, 1)]
+    facing = to((chip + CHIPS - 1 + 2 * core) % CHIPS, 1 - core)
+    greeted = [partner, facing]
     greeted += [peer_z(t) for t in range(1, 8)] + [peer_xy(t) for t in range(1, 16)]
     for other in greeted:
         pl.semaphore_signal(barrier, inc=1, device_id=other, device_id_type=MESH)
@@ -112,6 +111,8 @@
     )
     for item in loads[:6]:
         item.wait()
+    for item in loads[6:]:
+        item.start()
 
     def outer_layer(b, carry):
         span = pl.ds(pl.multiple_of(core * 448, 64), 64)
@@ -125,10 +126,8 @@
     pl.semaphore_wait(barrier, len(greeted))
     here = rows.at[core, xy, z]
     gather_z = go([remote(here, here, gz_sems, t, peer_z(t)) for t in range(1, 8)])
-    facing = (chip + CHIPS - 1 + 2 * core) % CHIPS
-    go([remote(halo_out, halo_in.at[1 - core], halo_sems, side, to(facing, side), 1 - core) for side in range(2)])
+    go([remote(halo_out, halo_in.at[1 - core], halo_sems, 0, facing, 1 - core)])
     swap_table = go([remote(own_table, other_table, pair_sems, 0, partner)])
-    swap_acts = go([remote(acts_hbm.at[pl.ds(8, 4)], acts.at[pl.ds(SLOTS, 4)], pair_sems, 1, partner)])
 
     def inner_layers(b, carry):
         for j in range(7):
@@ -154,19 +153,25 @@
                 mixed_table[i:i + 1, :] = jnp.where(foreign(i), other_table[15 - i:16 - i, :], own_table[i:i + 1, :])
             table_copy = pltpu.make_async_copy(mixed_table, table, table_sem)
             table_copy.start()
+    swap_acts = go([remote(acts_hbm.at[pl.ds(8, 4)], acts.at[pl.ds(SLOTS, 4)], pair_sems, 1, partner)])
     for item in loads[6:]:
         item.wait()
-    arrive(swap_acts)
-
-    def transpose_acts(i, carry):
-        brick = jnp.where(foreign(i), SLOTS + 7 - i, i)
+
+    def transpose_acts(i, brick):
         a = acts[brick].astype(F32).reshape(32, 2, 8, C)
         span = pl.ds(pl.multiple_of(i * 256, 256), 256)
         for parity in range(2):
             acts_t[parity * C:(parity + 1) * C, span] = a[:, parity].reshape(256, C).T.astype(BF16)
-        return carry
-
-    lax.fori_loop(0, ITEMS, transpose_acts, 0)
+
+    def lower_acts(i, carry):
+        transpose_acts(i, i)
+        return carry
+
+    def upper_acts(i, carry):
+        transpose_acts(i, jnp.where(foreign(i), SLOTS + 7 - i, i))
+        return carry
+
+    lax.fori_loop(0, 4, lower_acts, 0)
     table_copy.wait()
 
     row = lax.broadcasted_iota(jnp.int32, (1, 8, C), 1)
@@ -204,14 +209,21 @@
         return carry
 
     lax.fori_loop(0, 4, assemble_own, 0)
-    arrive(swap_g)
+    arrive(swap_g[:2])
 
     def widen(b, carry):
         grads[2 - core, b] = other_g[b].astype(F32).reshape(8, 8, 8, C)
         return carry
 
-    lax.fori_loop(0, SLOTS, widen, 0)
+    lax.fori_loop(0, 8, widen, 0)
+    arrive(swap_g[2:])
+    lax.fori_loop(8, SLOTS, widen, 0)
     lax.fori_loop(4, ITEMS, assemble_own, 0)
+    arrive(gather_z)
+    here = rows.at[core, xy]
+    gather_xy = go([remote(here, here, gxy_sems, t, peer_xy(t)) for t in range(1, 16)])
+    arrive(swap_acts)
+    lax.fori_loop(4, ITEMS, upper_acts, 0)
 
     def window(step_x, step_z, q, items):
         found = pads[2 - step_z, q, items, pl.ds(2 - step_x, 8), :, :]
@@ -261,14 +273,12 @@
                 remote(send1.at[target], recv1.at[xy], rxy_sems, target, to(target * 8 + z, core), xy).start()
 
     lax.fori_loop(0, 1, lambda step_z, carry: filter_terms(1, step_z, carry), 0)
-    arrive(gather_z)
-    here = rows.at[core, xy]
-    gather_xy = go([remote(here, here, gxy_sems, t, peer_xy(t)) for t in range(1, 16)])
+    remote(halo_out, halo_in.at[core], halo_sems, 0, partner, core).wait_recv()
+    go([remote(halo_in.at[core], halo_in.at[core], halo_sems, 1, partner, core)])
     lax.fori_loop(1, 3, lambda step_z, carry: filter_terms(1, step_z, carry), 0)
     reduce_pair = post_pair(0)
 
-    for side in range(2):
-        remote(halo_out, halo_in.at[side], halo_sems, 0, partner, side).wait_recv()
+    remote(halo_out, halo_in.at[1 - core], halo_sems, 0, partner, 1 - core).wait_recv()
 
     def widen_halo(b, carry):
         grads[0, b, 7] = halo_in[0, b].astype(F32).reshape(8, 8, C)
@@ -283,17 +293,18 @@
         return carry
 
     lax.fori_loop(0, ITEMS, assemble_halo, 0)
+    lax.fori_loop(0, 1, lambda step_z, carry: filter_terms(0, step_z, carry), 0)
     send_on(0, reduce_pair)
-    lax.fori_loop(0, 3, lambda step_z, carry: filter_terms(0, step_z, carry), 0)
+    lax.fori_loop(1, 3, lambda step_z, carry: filter_terms(0, step_z, carry), 0)
     reduce_pair = post_pair(1)
-    lax.fori_loop(0, 1, lambda step_z, carry: filter_terms(2, step_z, carry), 0)
+    lax.fori_loop(0, 2, lambda step_z, carry: filter_terms(2, step_z, carry), 0)
     send_on(1, reduce_pair)
-    lax.fori_loop(1, 3, lambda step_z, carry: filter_terms(2, step_z, carry), 0)
+    lax.fori_loop(2, 3, lambda step_z, carry: filter_terms(2, step_z, carry), 0)
     reduce_pair = post_pair(2)
+    send_on(2, reduce_pair)
     arrive(gather_xy)
     here = rows.at[core]
     gather_last = go([remote(here, here, gp_sems, 0, partner)])
-    send_on(2, reduce_pair)
 
     arrive(gather_last)
 
@@ -338,14 +349,6 @@
         both = jnp.stack([total[:, :, :C], total[:, :, C:]], axis=1)
         return both.reshape(2, VOX, C)
 
-    stores = []
-
-    def store(part):
-        span = pl.ds(part * 4, 4)
-        item = pltpu.make_async_copy(in_grad.at[span], in_grad_hbm.at[span], store_sem.at[part])
-        item.start()
-        stores.append(item)
-
     def upper_items(pair, carry):
         found = input_terms(pair)
         for k in range(2):
@@ -356,8 +359,7 @@
         return carry
 
     lax.fori_loop(2, 4, upper_items, 0)
-    give_back = go([remote(returned, in_grad.at[pl.ds(8, 4)], pair_sems, 3, partner)])
-    store(1)
+    give_back = go([remote(returned, landed, pair_sems, 3, partner)])
 
     for source in range(16):
         @pl.when(source != xy)
@@ -376,9 +378,9 @@
         return carry
 
     lax.fori_loop(0, 2, lower_items, 0)
-    store(0)
     arrive(give_back)
-    store(2)
+    place = pltpu.make_async_copy(landed, in_grad.at[pl.ds(8, 4)], store_sem)
+    place.start()
 
     arrive(reduce_z)
     total = sum1[xy, z]
@@ -387,8 +389,7 @@
     total = total * (1.0 / math.sqrt(BRICKS * VOX))
     filt_grad_ref[0:16, :] = total[:, 0:64]
     filt_grad_ref[16:27, :] = total[0:11, 64:128]
-    for item in stores:
-        item.wait()
+    place.wait()
     for item in started:
         item.wait_send()
     for target in range(16):
@@ -397,34 +398,20 @@
             remote(send1.at[target], recv1.at[target], rxy_sems, target, partner).wait_send()
 
 
-def hand_over(source, filt_ref, target, filt_out, buffer, in_sem, out_sem):
-    parts = [pl.ds(k * 4, 4) for k in range(3)]
-    reads = [pltpu.make_async_copy(source.at[p], buffer.at[p], in_sem.at[k]) for k, p in enumerate(parts)]
-    writes = [pltpu.make_async_copy(buffer.at[p], target.at[p], out_sem.at[k]) for k, p in enumerate(parts)]
-    for item in reads:
-        item.start()
-    filt_out[...] = filt_ref[...]
-    for k in range(3):
-        reads[k].wait()
-        writes[k].start()
-    for item in writes:
-        item.wait()
-
-
 def on_device(acts, preact, cotangent, filt, counts, neighbors):
     vmem, dma = pltpu.VMEM, pltpu.SemaphoreType.DMA
     any_space = pl.BlockSpec(memory_space=pl.ANY)
     in_smem = pl.BlockSpec(memory_space=pltpu.SMEM)
     in_vmem = pl.BlockSpec(memory_space=pltpu.VMEM)
     out_shape = (
-        jax.ShapeDtypeStruct((SLOTS, VOX, C), BF16),
-        jax.ShapeDtypeStruct((27, 64), F32),
+        pltpu.VMEM((SLOTS, VOX, C), BF16),
+        pltpu.VMEM((27, 64), F32),
     )
     found = pl.pallas_call(
         kernel,
         out_shape=out_shape,
         in_specs=[in_smem, in_vmem, any_space, any_space, any_space, in_vmem],
-        out_specs=(any_space, in_vmem),
+        out_specs=(in_vmem, in_vmem),
         scratch_shapes=[
             vmem((SLOTS + 4, VOX, C), BF16),
             vmem((SLOTS, VOX, C), BF16),
@@ -451,9 +438,9 @@
             vmem((16, 8, 16, C), BF16),
             vmem((8, 16, C), BF16),
             vmem((7, 16, C), BF16),
-            vmem((SLOTS, VOX, C), BF16),
             vmem((4, VOX, C), BF16),
-            dma((9,)), dma((3,)), dma(()), dma((2, 8)), dma((2, 2)), dma((2, 8)), dma((2, 16)), dma((2, 1)),
+            vmem((4, VOX, C), BF16),
+            dma((9,)), dma(()), dma(()), dma((2, 8)), dma((2, 2)), dma((2, 8)), dma((2, 16)), dma((2, 1)),
             dma((2, 3)), dma((2, 16)), dma((2, 8)),
         ],
         compiler_params=pltpu.CompilerParams(
@@ -461,14 +448,7 @@
         ),
         name="brick_backward",
     )(counts, neighbors, acts, preact, cotangent, filt)
-    return pl.pallas_call(
-        hand_over,
-        out_shape=out_shape,
-        in_specs=[any_space, in_vmem],
-        out_specs=(any_space, in_vmem),
-        scratch_shapes=[vmem((SLOTS, VOX, C), BF16), dma((3,)), dma((3,))],
-        name="hand_over",
-    )(*found)
+    return found
 
 
 def solution(mesh):

time: 46.3 us -> 43.1 us (0.931)
  the two profiles are of different devices: /device:TPU:30 before, /device:TPU:1 now
where the time goes in v5:
time: 43.1 us; the launch traced here: 42.3 us
  Pallas kernels  39.9 us (93%)
  local copies, waits for them, and re-layouts  1.75 us (4%)
  between operations  0.64 us (1%)
    pallas_call x1, Pallas kernels, on_device(): pl.pallas_call(kernel, out_shape=out_shape, in_specs=[in_smem, in_vmem, a...  39.9 us
    unnamed x2, local copies, waits for them, and re-layouts  1.75 us

profile of v5, /device:TPU:1, one launch (start us, length us, event | category | flops | bytes accessed | tf_op | source)
XLA Modules:
  0.0 42.3 jit_solution(4110333380605720949)
XLA Ops:
  0.6 39.9 %brick_backward.1 = (bf16[12,512,128]{2,1,0:T(8,128)(2,1)S(1)}, f32[27,64]{1,0:T(8,128)S(1)}) custom-call(s32[256]{0:T(256)} %counts.1, s32[12,27]{1,0:T(8,128)} %neighbors.1, bf16[12,512,128]{2,1,0:T(8,128)(2,1)} %acts_hbm.1, bf16[12,512,128]{2,1,0:T(8,128)(2,1)} %pre_hbm.1, bf16[12,512,128]{2,1,0:T(8,128)(2,1)} %cot_hbm.1, bf16[27,64]{1,0:T(8,128)(2,1)} %filt_ref.1), custom_call_target="tpu_custom_call" | custom-call | tf_op jit(solution)/shard_map/brick_backward/pallas_call | solution.py:410
  40.5 1.1 %copy.10 = bf16[12,512,128]{2,1,0:T(8,128)(2,1)} copy(bf16[12,512,128]{2,1,0:T(8,128)(2,1)S(1)} %get-tuple-element.2) | data formatting | bytes 3145728
  41.7 0.6 %copy.11 = f32[27,64]{1,0:T(8,128)} copy(f32[27,64]{1,0:T(8,128)S(1)} %get-tuple-element.3) | data formatting | bytes 13824

commit v6 on v5

--- a/solution.py
+++ b/solution.py
@@ -275,7 +275,7 @@
     lax.fori_loop(0, 1, lambda step_z, carry: filter_terms(1, step_z, carry), 0)
     remote(halo_out, halo_in.at[core], halo_sems, 0, partner, core).wait_recv()
     go([remote(halo_in.at[core], halo_in.at[core], halo_sems, 1, partner, core)])
-    lax.fori_loop(1, 3, lambda step_z, carry: filter_terms(1, step_z, carry), 0)
+    lax.fori_loop(1, 3, lambda step_z, carry: filter_terms(1, step_z, carry), 0, unroll=True)
     reduce_pair = post_pair(0)
 
     remote(halo_out, halo_in.at[1 - core], halo_sems, 0, partner, 1 - core).wait_recv()
@@ -295,9 +295,9 @@
     lax.fori_loop(0, ITEMS, assemble_halo, 0)
     lax.fori_loop(0, 1, lambda step_z, carry: filter_terms(0, step_z, carry), 0)
     send_on(0, reduce_pair)
-    lax.fori_loop(1, 3, lambda step_z, carry: filter_terms(0, step_z, carry), 0)
+    lax.fori_loop(1, 3, lambda step_z, carry: filter_terms(0, step_z, carry), 0, unroll=True)
     reduce_pair = post_pair(1)
-    lax.fori_loop(0, 2, lambda step_z, carry: filter_terms(2, step_z, carry), 0)
+    lax.fori_loop(0, 2, lambda step_z, carry: filter_terms(2, step_z, carry), 0, unroll=True)
     send_on(1, reduce_pair)
     lax.fori_loop(2, 3, lambda step_z, carry: filter_terms(2, step_z, carry), 0)
     reduce_pair = post_pair(2)

time: 43.1 us -> 42.9 us (level)
  the two profiles are of different devices: /device:TPU:1 before, /device:TPU:19 now
where the time goes in v6:
time: 42.9 us; the launch traced here: 42.8 us
  Pallas kernels  40.4 us (94%)
  local copies, waits for them, and re-layouts  1.75 us (4%)
  between operations  0.64 us (1%)
    pallas_call x1, Pallas kernels, on_device(): pl.pallas_call(kernel, out_shape=out_shape, in_specs=[in_smem, in_vmem, a...  40.4 us
    unnamed x2, local copies, waits for them, and re-layouts  1.75 us

profile of v6, /device:TPU:19, one launch (start us, length us, event | category | flops | bytes accessed | tf_op | source)
XLA Modules:
  0.0 42.8 jit_solution(6163599280523653966)
XLA Ops:
  0.6 40.4 %brick_backward.1 = (bf16[12,512,128]{2,1,0:T(8,128)(2,1)S(1)}, f32[27,64]{1,0:T(8,128)S(1)}) custom-call(s32[256]{0:T(256)} %counts.1, s32[12,27]{1,0:T(8,128)} %neighbors.1, bf16[12,512,128]{2,1,0:T(8,128)(2,1)} %acts_hbm.1, bf16[12,512,128]{2,1,0:T(8,128)(2,1)} %pre_hbm.1, bf16[12,512,128]{2,1,0:T(8,128)(2,1)} %cot_hbm.1, bf16[27,64]{1,0:T(8,128)(2,1)} %filt_ref.1), custom_call_target="tpu_custom_call" | custom-call | tf_op jit(solution)/shard_map/brick_backward/pallas_call | solution.py:410
  41.1 1.1 %copy.10 = bf16[12,512,128]{2,1,0:T(8,128)(2,1)} copy(bf16[12,512,128]{2,1,0:T(8,128)(2,1)S(1)} %get-tuple-element.2) | data formatting | bytes 3145728
  42.2 0.6 %copy.11 = f32[27,64]{1,0:T(8,128)} copy(f32[27,64]{1,0:T(8,128)S(1)} %get-tuple-element.3) | data formatting | bytes 13824
